TPU v7x, 128 devices: a whole 4x4x4 slice. The times are simulated.
128 devices in a mesh: dp: 8 (over x, core), blk: 16 (over z, y).
Axes of the slice: x: 4, y: 4, z: 4, core: 2. Of those that a mesh axis runs over, the one named last changes fastest.
Arguments:
- rows: bfloat16 [131072, 768], P(('dp', 'blk')), may hold values from -6 to 6
- block_ids: int32 [131072, 1], P(('dp', 'blk')), may hold values from 0 to 127; in each aligned block of 1024 rows (0 to 1023, 1024 to 2047, ...) at most 16 rows name the same one
- centroids: float32 [131072, 768], P(('dp', 'blk')), may hold values from -6 to 6
- pairing: int32 [2], replicated, may hold values from 1 to 15
Outputs:
- centers: float32 [131072, 768], P(('dp', 'blk'))
- energy: float32 [131072], P(('dp', 'blk'))
Inputs may be any that keep to these rules, and one draw needn't show every extreme that they name: Row r belongs to the block owned by the device of flat index block_ids[r, 0] over dp+blk with dp slowest; among the rows of one device no id occurs more than 16 times, and that many is reached in every draw. In pass p, the blocks at positions k and k XOR pairing[p] of one group are partners.
All inputs are finite; a program needn't handle non-finite values.
Results may differ from a plain program's by a relative error of at most 0.007.
Values may be sent and summed in bfloat16 or wider, within the bound.
No kernel may reach another device: no remote copies, remote signals or barrier semaphores. Data moves between devices by JAX's collectives and lax.ppermute only.
A program may use at most 64 MiB of HBM per device.

v0:
```python
import math

import jax
import jax.numpy as jnp
from jax import lax
from jax.sharding import PartitionSpec as P

PASSES = 2
KAPPA = 64.0
ABSENT = 1.25
LIMIT = 1.125


def unit_vectors(values):
    wide = values.astype(jnp.float32)
    scale = lax.rsqrt(jnp.mean(wide * wide, axis=-1, keepdims=True) + 1e-06) * values.shape[-1] ** (
        -0.5
    )
    return (wide * scale).astype(jnp.bfloat16)


def contract_rows(left, right):
    return lax.dot_general(
        left, right, (((1,), (1,)), ((), ())), preferred_element_type=jnp.float32
    )


def contract_cols(left, right):
    return lax.dot_general(
        left, right, (((1,), (0,)), ((), ())), preferred_element_type=jnp.float32
    )


def partner_swap(value, mask, width):
    def branch(apart):
        if apart == 0:
            return lambda current: current
        return lambda current: lax.ppermute(current, "blk", [(i, i ^ apart) for i in range(width)])

    return lax.switch(mask, [branch(apart) for apart in range(width)], value)


def on_device(rows, block_ids, centroids, pairing):
    groups = lax.axis_size("dp")
    group_width = lax.axis_size("blk")
    devices = groups * group_width
    rows_dev, width = rows.shape
    tile_rows = centroids.shape[0]
    capacity = 2 * rows_dev // devices
    slot_count = devices * capacity
    owners = block_ids[:, 0]
    indicator = (owners[:, None] == jnp.arange(devices, dtype=jnp.int32)[None, :]).astype(jnp.int32)
    earlier = jnp.cumsum(indicator, axis=0, dtype=jnp.int32) - indicator
    place = jnp.sum(earlier * indicator, axis=1, dtype=jnp.int32)
    position = owners * capacity + place
    unit_rows = unit_vectors(rows)
    blank = jnp.where(jnp.arange(width)[None, :] == 0, ABSENT, 0.0).astype(jnp.bfloat16)
    outgoing = jnp.broadcast_to(blank, (slot_count, width)).at[position].set(unit_rows)
    chunks = outgoing.reshape(groups, group_width, capacity, width)

    def routed(mask):
        order = jnp.bitwise_xor(jnp.arange(group_width, dtype=jnp.int32), mask)
        sent = jnp.take(chunks, order, axis=1).reshape(devices, capacity, width)
        got = lax.all_to_all(sent, ("dp", "blk"), split_axis=0, concat_axis=0, tiled=True)
        return got.reshape(slot_count, width)

    own = lax.all_to_all(
        chunks.reshape(devices, capacity, width),
        ("dp", "blk"),
        split_axis=0,
        concat_axis=0,
        tiled=True,
    ).reshape(slot_count, width)
    others = [routed(pairing[p]) for p in range(PASSES)]
    own_here = own[:, 0] < LIMIT
    centers = centroids
    for p in range(PASSES):
        unit_tiles = unit_vectors(centers)
        other = others[p]
        other_here = other[:, 0] < LIMIT
        own_aff = jnp.exp(KAPPA * contract_rows(unit_tiles, own))
        other_aff = jnp.exp(KAPPA * contract_rows(unit_tiles, other))
        partial = jnp.stack([jnp.sum(own_aff, axis=0), jnp.sum(other_aff, axis=0)])
        swapped = partner_swap(partial, pairing[p], group_width)
        totals = partial[0] + swapped[1]
        other_totals = partial[1] + swapped[0]
        own_w = (own_aff * jnp.where(own_here, 1.0 / totals, 0.0)[None, :]).astype(jnp.bfloat16)
        other_w = (other_aff * jnp.where(other_here, 1.0 / other_totals, 0.0)[None, :]).astype(
            jnp.bfloat16
        )
        numerator = contract_cols(own_w, own) + contract_cols(other_w, other)
        counts = jnp.sum(own_w.astype(jnp.float32), axis=1) + jnp.sum(
            other_w.astype(jnp.float32), axis=1
        )
        centers = (
            math.sqrt(width)
            * (numerator + unit_tiles.astype(jnp.float32))
            / (counts + 1.0)[:, None]
        )
    slot_energy = jnp.log(totals / (2.0 * tile_rows))
    returned = lax.all_to_all(
        slot_energy.reshape(devices, capacity),
        ("dp", "blk"),
        split_axis=0,
        concat_axis=0,
        tiled=True,
    )
    energy = returned.reshape(slot_count)[position]
    return (centers, energy)


def solution(mesh):
    in_specs = (P(("dp", "blk"), None), P(("dp", "blk"), None), P(("dp", "blk"), None), P())
    out_specs = (P(("dp", "blk"), None), P(("dp", "blk")))
    return jax.shard_map(
        on_device, mesh=mesh, in_specs=in_specs, out_specs=out_specs, check_vma=False
    )
```

profile of v0, /device:TPU:1, one launch (start us, length us, event | category | flops | bytes accessed | tf_op | source)
XLA Modules:
  0.0 269.8 jit_solution(5146993017238362431)
XLA Ops:
  6.0 1.9 broadcast_in_dim.44
  7.9 9.6 %scatter_custom_fusion = bf16[2048,768]{1,0:T(8,128)(2,1)} fusion(bf16[2048,768]{1,0:T(8,128)(2,1)} %broadcast_in_dim.44, s32[1024]{0:T(1024)S(1)} %bitcast.78, bf16[1024,768]{1,0:T(8,128)(2,1)S(1)} %copy-done.3, f32[1024]{0:T(1024)S(1)} %rsqrt_multiply_fusion.1), kind=kCustom, calls=%fused_computation.32 | custom fusion | flops 2359296 | bytes 4722688 | tf_op jit(solution)/shard_map/scatter | solution.py:58
  17.5 2.6 gather_fusion.1
  20.8 51.6 %all_to_all.21 = bf16[128,16,768]{2,1,0:T(8,128)(2,1)} all-to-all(bf16[128,16,768]{2,1,0:T(8,128)(2,1)S(1)} %bitcast.48), channel_id=1, replica_groups=mesh['dp'=8,'blk'=16] {'dp','blk'}, dimensions={0} | all-to-all | bytes 6291456 | tf_op jit(solution)/shard_map/all_to_all | solution.py:64
  72.4 18.0 %all-to-all-start = ((bf16[128,16,768]{2,1,0:T(8,128)(2,1)}), bf16[128,16,768]{2,1,0:T(8,128)(2,1)}, u32[]{:S(2)}, u32[]{:S(2)}) async-start(bf16[128,16,768]{2,1,0:T(8,128)(2,1)} %bitcast.7), calls=%async_computation | async-start | bytes 6291456 | tf_op jit(solution)/shard_map/all_to_all | solution.py:67
  90.4 2.3 copy.28
  94.7 4.3 %gather_fusion.2 = bf16[16,8,16,768]{3,2,1,0:T(8,128)(2,1)} fusion(bf16[8,16,16,768]{3,2,1,0:T(8,128)(2,1)} %bitcast.11, s32[1024]{0:T(1024)S(1)} %pad_clamp_fusion), kind=kCustom, calls=%fused_computation.1.clone | custom fusion | bytes 6291520 | tf_op jit(solution)/shard_map/jit(_take)/gather | solution.py:63
  99.7 2.3 select_bitcast_fusion
  102.0 2.0 copy.32
  104.3 1.6 copy-done.1
  107.4 5.9 %fusion.1 = (f32[2048]{0:T(1024)S(1)}, f32[1024,2048]{1,0:T(8,128)}) fusion(bf16[1024,768]{0,1:T(8,128)(2,1)S(1)} %multiply_convert_fusion.5, bf16[2048,768]{1,0:T(8,128)(2,1)S(1)} %bitcast.58), kind=kOutput, calls=%fused_computation.17 | convolution fusion | flops 3225417728 | bytes 13115392 | tf_op jit(solution)/shard_map/dot_general | solution.py:23
  113.3 16.9 %all-to-all-done = bf16[128,16,768]{2,1,0:T(8,128)(2,1)} async-done(((bf16[128,16,768]{2,1,0:T(8,128)(2,1)}), bf16[128,16,768]{2,1,0:T(8,128)(2,1)}, u32[]{:S(2)}, u32[]{:S(2)}) %all-to-all-start) | async-done | bytes 3145760 | tf_op jit(solution)/shard_map/all_to_all | solution.py:67
  130.3 5.3 %all-to-all-start.2 = ((bf16[128,16,768]{2,1,0:T(8,128)(2,1)}), bf16[128,16,768]{2,1,0:T(8,128)(2,1)S(1)}, u32[]{:S(2)}, u32[]{:S(2)}) async-start(bf16[128,16,768]{2,1,0:T(8,128)(2,1)} %bitcast.21), calls=%async_computation.2 | async-start | bytes 6291456 | tf_op jit(solution)/shard_map/all_to_all | solution.py:64
  135.6 9.4 %fusion = (f32[2048]{0:T(1024)S(1)}, f32[1024,2048]{1,0:T(8,128)}) fusion(bf16[1024,768]{0,1:T(8,128)(2,1)} %copy-done.7, bf16[2048,768]{1,0:T(8,128)(2,1)} %bitcast.8), kind=kOutput, calls=%fused_computation.16 | convolution fusion | flops 3225417728 | bytes 13115392 | tf_op jit(solution)/shard_map/dot_general | solution.py:23
  145.1 1.4 compare_reduce_fusion.2
  146.5 26.0 %conditional.2 = (f32[2,2048]{1,0:T(2,128)S(1)}) conditional(s32[]{:T(128)} %clamp.6, f32[2,2048]{1,0:T(2,128)S(1)} %pad_maximum_fusion, f32[2,2048]{1,0:T(2,128)S(1)} %pad_maximum_fusion, f32[2,2048]{1,0:T(2,128)S(1)} %pad_maximum_fusion, f32[2,2048]{1,0:T(2,128)S(1)} %pad_maximum_fusion, ...), branch_computations={%region_8.10_spmd, %region_9.11_spmd, %region_10.12_spmd, %region_... | conditional | bytes 98352 | solution.py:40
  146.5 5.9 %collective-permute-start.13 = (f32[2,2048]{1,0:T(2,128)S(1)}, f32[2,2048]{1,0:T(2,128)S(1)}, u32[]{:S(2)}, u32[]{:S(2)}) collective-permute-start(f32[2,2048]{1,0:T(2,128)S(1)} %param.16), channel_id=1, source_target_pairs={{0,14},{1,15},{2,12},{3,13},{4,10},{5,11},{6,8},{7,9},{8,6},{9,7},... | collective-permute-start | bytes 49160 | tf_op jit(solution)/shard_map/cond/branch_14_fun/ppermute | solution.py:38
  152.4 20.0 %collective-permute-done.13 = f32[2,2048]{1,0:T(2,128)S(1)} collective-permute-done((f32[2,2048]{1,0:T(2,128)S(1)}, f32[2,2048]{1,0:T(2,128)S(1)}, u32[]{:S(2)}, u32[]{:S(2)}) %collective-permute-start.13) | collective-permute-done | bytes 16416 | tf_op jit(solution)/shard_map/cond/branch_14_fun/ppermute | solution.py:38
  172.5 9.6 %fusion.9 = f32[1024,768]{0,1:T(8,128)} fusion(bf16[2048,768]{1,0:T(8,128)(2,1)} %bitcast.8, f32[1024,2048]{1,0:T(8,128)} %get-tuple-element.87, f32[2048]{0:T(1024)S(1)} %bitcast.69), kind=kOutput, calls=%fused_computation.37 | convolution fusion | flops 3227516928 | bytes 14688256 | tf_op jit(solution)/shard_map/dot_general | solution.py:29
  182.1 3.3 %convert_reduce_fusion.2 = (f32[1024]{0:T(1024)S(1)}, f32[1024]{0:T(1024)S(1)}) fusion(f32[2048]{0:T(1024)S(1)} %bitcast.67, f32[1024,2048]{1,0:T(8,128)S(1)} %bitcast.50, f32[2048]{0:T(1024)S(1)} %bitcast.70, f32[1024,2048]{1,0:T(8,128)S(1)} %bitcast.52), kind=kLoop, calls=%fused_computation.10 | loop fusion | flops 20969472 | bytes 16801792 | tf_op jit(solution)/shard_map/reduce_sum | solution.py:92
  185.5 7.1 %multiply_reduce_fusion = (f32[1024]{0:T(1024)S(1)}, f32[1024,768]{0,1:T(8,128)S(1)}) fusion(f32[1024]{0:T(1024)S(1)} %add_add_fusion.1, bf16[1024,768]{0,1:T(8,128)(2,1)S(1)} %copy-done.8, f32[1024,768]{0,1:T(8,128)} %fusion.9, bf16[2048,768]{1,0:T(8,128)(2,1)} %bitcast.56, f32[1024,2048]{1,0:T(8,128)S(1)} %bitcast.50, f32[2048]{0:T(1024)S(1)} %bitcast.68), kind=kOutput, calls=%fused_computation.28 | convolution fusion | flops 3233020928 | bytes 19415040 | tf_op jit(solution)/shard_map/dot_general | solution.py:29
  194.2 7.9 %fusion.2 = (f32[2048]{0:T(1024)S(1)}, f32[1024,2048]{1,0:T(8,128)}) fusion(bf16[1024,768]{0,1:T(8,128)(2,1)S(1)} %multiply_convert_fusion.4, bf16[2048,768]{1,0:T(8,128)(2,1)} %bitcast.8), kind=kOutput, calls=%fused_computation.18 | convolution fusion | flops 3225417728 | bytes 13115392 | tf_op jit(solution)/shard_map/dot_general | solution.py:23
  202.1 7.3 %fusion.3 = (f32[2048]{0:T(1024)S(1)}, f32[1024,2048]{1,0:T(8,128)}) fusion(bf16[1024,768]{0,1:T(8,128)(2,1)} %copy-done.5, bf16[2048,768]{1,0:T(8,128)(2,1)S(1)} %bitcast.53), kind=kOutput, calls=%fused_computation.19 | convolution fusion | flops 3225417728 | bytes 13115392 | tf_op jit(solution)/shard_map/dot_general | solution.py:23
  209.8 6.5 %conditional.3 = (f32[2,2048]{1,0:T(2,128)S(1)}) conditional(s32[]{:T(128)} %clamp.7, f32[2,2048]{1,0:T(2,128)S(1)} %pad_maximum_fusion.1, f32[2,2048]{1,0:T(2,128)S(1)} %pad_maximum_fusion.1, f32[2,2048]{1,0:T(2,128)S(1)} %pad_maximum_fusion.1, f32[2,2048]{1,0:T(2,128)S(1)} %pad_maximum_fusion.1, ...), branch_computations={%region_29.31_spmd, %region_30.32_spmd, %region_31.33_spmd, %regio... | conditional | bytes 98352 | solution.py:40
  210.1 6.2 %collective-permute-done.25 = f32[2,2048]{1,0:T(2,128)S(1)} collective-permute-done((f32[2,2048]{1,0:T(2,128)S(1)}, f32[2,2048]{1,0:T(2,128)S(1)}, u32[]{:S(2)}, u32[]{:S(2)}) %collective-permute-start.25) | collective-permute-done | bytes 16416 | tf_op jit(solution)/shard_map/cond/branch_11_fun/ppermute | solution.py:38
  216.4 5.0 %convert_reduce_fusion.1 = f32[1024]{0:T(1024)S(1)} fusion(f32[2048]{0:T(1024)S(1)} %bitcast.65, f32[1024,2048]{1,0:T(8,128)} %get-tuple-element.93), kind=kLoop, calls=%fused_computation.5 | loop fusion | flops 10484736 | bytes 8400896 | tf_op jit(solution)/shard_map/reduce_sum | solution.py:92
  222.1 7.0 %fusion.10 = f32[1024,768]{0,1:T(8,128)} fusion(bf16[2048,768]{1,0:T(8,128)(2,1)} %bitcast.8, f32[1024,2048]{1,0:T(8,128)S(1)} %copy-done.2, f32[2048]{0:T(1024)S(1)} %bitcast.66), kind=kOutput, calls=%fused_computation.38 | convolution fusion | flops 3227516928 | bytes 14688256 | tf_op jit(solution)/shard_map/dot_general | solution.py:29
  229.9 10.1 %all-to-all-start.3 = ((f32[128,1,16]{2,1,0:T(1,128)}), f32[128,1,16]{2,1,0:T(1,128)S(1)}, u32[]{:S(2)}, u32[]{:S(2)}) async-start(f32[128,1,16]{2,1,0:T(1,128)} %bitcast.26), calls=%async_computation.3 | async-start | bytes 131072 | tf_op jit(solution)/shard_map/all_to_all | solution.py:101
  240.1 5.0 %convert_reduce_fusion = f32[1024]{0:T(1024)S(1)} fusion(f32[2048]{0:T(1024)S(1)} %bitcast.63, f32[1024,2048]{1,0:T(8,128)} %get-tuple-element.91), kind=kLoop, calls=%fused_computation.4 | loop fusion | flops 10484736 | bytes 8400896 | tf_op jit(solution)/shard_map/reduce_sum | solution.py:92
  245.1 9.0 %multiply_divide_fusion = f32[1024,768]{0,1:T(8,128)} fusion(bf16[1024,768]{0,1:T(8,128)(2,1)S(1)} %copy-done.6, f32[1024,768]{0,1:T(8,128)S(1)} %copy-done.10, bf16[2048,768]{1,0:T(8,128)(2,1)S(1)} %bitcast.55, f32[1024]{0:T(1024)S(1)} %add_add_fusion, f32[1024,2048]{1,0:T(8,128)} %get-tuple-element.91, f32[2048]{0:T(1024)S(1)} %bitcast.64), kind=kOutput, calls=%fused_computation.26 | convolution fusion | flops 3231449088 | bytes 19410944 | tf_op jit(solution)/shard_map/dot_general | solution.py:29
  254.1 3.5 %copy.36 = f32[1024,768]{1,0:T(8,128)} copy(f32[1024,768]{0,1:T(8,128)} %multiply_divide_fusion) | data formatting | bytes 6291456
  259.0 10.5 %gather_fusion = f32[1024]{0:T(1024)} fusion(f32[2048]{0:T(1024)S(1)} %reshape.175, s32[1024]{0:T(1024)S(1)} %broadcast_clamp_fusion), kind=kCustom, calls=%fused_computation.2 | custom fusion | bytes 12288 | tf_op jit(solution)/shard_map/gather | solution.py:108
  (77 shorter events, 14.3 us)
Async XLA Ops:
  0.6 4.9 %copy-start.9 = (s32[1024,1]{0,1:T(1,128)S(1)}, s32[1024,1]{0,1:T(1,128)}, u32[]{:S(2)}) copy-start(s32[1024,1]{0,1:T(1,128)} %param.39) | copy-start | bytes 12292
  0.6 5.0 %copy-start.3 = (bf16[1024,768]{1,0:T(8,128)(2,1)S(1)}, bf16[1024,768]{1,0:T(8,128)(2,1)}, u32[]{:S(2)}) copy-start(bf16[1024,768]{1,0:T(8,128)(2,1)} %param.38) | copy-start | bytes 4718596
  72.4 18.0 %copy-start = (f32[1024,768]{1,0:T(8,128)S(1)}, f32[1024,768]{1,0:T(8,128)}, u32[]{:S(2)}) copy-start(f32[1024,768]{1,0:T(8,128)} %param.40) | copy-start | bytes 9437188
  72.4 57.9 %all-to-all-start = ((bf16[128,16,768]{2,1,0:T(8,128)(2,1)}), bf16[128,16,768]{2,1,0:T(8,128)(2,1)}, u32[]{:S(2)}, u32[]{:S(2)}) async-start(bf16[128,16,768]{2,1,0:T(8,128)(2,1)} %bitcast.7), calls=%async_computation | async-start | bytes 6291456 | tf_op jit(solution)/shard_map/all_to_all | solution.py:67
  104.0 1.9 copy-start.1
  104.2 2.6 copy-start.4
  106.3 1.2 copy-start.7
  130.3 71.8 %all-to-all-start.2 = ((bf16[128,16,768]{2,1,0:T(8,128)(2,1)}), bf16[128,16,768]{2,1,0:T(8,128)(2,1)S(1)}, u32[]{:S(2)}, u32[]{:S(2)}) async-start(bf16[128,16,768]{2,1,0:T(8,128)(2,1)} %bitcast.21), calls=%async_computation.2 | async-start | bytes 6291456 | tf_op jit(solution)/shard_map/all_to_all | solution.py:64
  146.5 25.9 %collective-permute-start.13 = (f32[2,2048]{1,0:T(2,128)S(1)}, f32[2,2048]{1,0:T(2,128)S(1)}, u32[]{:S(2)}, u32[]{:S(2)}) collective-permute-start(f32[2,2048]{1,0:T(2,128)S(1)} %param.16), channel_id=1, source_target_pairs={{0,14},{1,15},{2,12},{3,13},{4,10},{5,11},{6,8},{7,9},{8,6},{9,7},... | collective-permute-start | bytes 49160 | tf_op jit(solution)/shard_map/cond/branch_14_fun/ppermute | solution.py:38
  172.5 9.6 %slice-start = ((s8[8388608]{0:T(1024)(128)(4,1)}), s8[4194304]{0:T(1024)(128)(4,1)S(1)}, s32[]{:S(2)}) async-start(s8[8388608]{0:T(1024)(128)(4,1)} %bitcast.49), calls=%async_computation.4 | async-start | bytes 8388608
  172.5 9.6 %slice-start.2 = ((s8[8388608]{0:T(1024)(128)(4,1)}), s8[4194304]{0:T(1024)(128)(4,1)S(1)}, s32[]{:S(2)}) async-start(s8[8388608]{0:T(1024)(128)(4,1)} %bitcast.51), calls=%async_computation.6 | async-start | bytes 8388608
  172.5 9.6 %slice-start.1 = ((s8[8388608]{0:T(1024)(128)(4,1)}), s8[4194304]{0:T(1024)(128)(4,1)S(1)}, s32[]{:S(2)}) async-start(s8[8388608]{0:T(1024)(128)(4,1)} %bitcast.49), calls=%async_computation.5 | async-start | bytes 8388608
  172.5 9.6 %slice-start.3 = ((s8[8388608]{0:T(1024)(128)(4,1)}), s8[4194304]{0:T(1024)(128)(4,1)S(1)}, s32[]{:S(2)}) async-start(s8[8388608]{0:T(1024)(128)(4,1)} %bitcast.51), calls=%async_computation.7 | async-start | bytes 8388608
  182.1 3.3 %copy-start.8 = (bf16[1024,768]{0,1:T(8,128)(2,1)S(1)}, bf16[1024,768]{0,1:T(8,128)(2,1)}, u32[]{:S(2)}) copy-start(bf16[1024,768]{0,1:T(8,128)(2,1)} %copy-done.7) | copy-start | bytes 4718596
  193.0 1.2 copy-start.5
  210.0 6.3 %collective-permute-start.25 = (f32[2,2048]{1,0:T(2,128)S(1)}, f32[2,2048]{1,0:T(2,128)S(1)}, u32[]{:S(2)}, u32[]{:S(2)}) collective-permute-start(f32[2,2048]{1,0:T(2,128)S(1)} %param.29), channel_id=1, source_target_pairs={{0,11},{1,10},{2,9},{3,8},{4,15},{5,14},{6,13},{7,12},{8,3},{9,2},... | collective-permute-start | bytes 49160 | tf_op jit(solution)/shard_map/cond/branch_11_fun/ppermute | solution.py:38
  216.4 5.8 %copy-start.2 = (f32[1024,2048]{1,0:T(8,128)S(1)}, f32[1024,2048]{1,0:T(8,128)}, u32[]{:S(2)}) copy-start(f32[1024,2048]{1,0:T(8,128)} %get-tuple-element.93) | copy-start | bytes 25165828
  229.9 27.7 %all-to-all-start.3 = ((f32[128,1,16]{2,1,0:T(1,128)}), f32[128,1,16]{2,1,0:T(1,128)S(1)}, u32[]{:S(2)}, u32[]{:S(2)}) async-start(f32[128,1,16]{2,1,0:T(1,128)} %bitcast.26), calls=%async_computation.3 | async-start | bytes 131072 | tf_op jit(solution)/shard_map/all_to_all | solution.py:101
  240.1 5.0 %copy-start.6 = (bf16[1024,768]{0,1:T(8,128)(2,1)S(1)}, bf16[1024,768]{0,1:T(8,128)(2,1)}, u32[]{:S(2)}) copy-start(bf16[1024,768]{0,1:T(8,128)(2,1)} %copy-done.5) | copy-start | bytes 4718596
  240.1 5.0 %copy-start.10 = (f32[1024,768]{0,1:T(8,128)S(1)}, f32[1024,768]{0,1:T(8,128)}, u32[]{:S(2)}) copy-start(f32[1024,768]{0,1:T(8,128)} %fusion.10) | copy-start | bytes 9437188
where the time goes:
time: 271 us; the launch traced here: 270 us
  matrix products  63.2 us (23%)
  blocking collectives  51.6 us (19%)
  waiting for transfers between devices  43.2 us (16%)
  starting transfers between devices  39.4 us (15%)
  local copies, waits for them, and re-layouts  34.9 us (13%)
  other arithmetic  34.6 us (13%)
    all_to_all x1, blocking collectives, routed(): lax.all_to_all(sent, ('dp', 'blk'), split_axis=0, concat_axis=0, tiled=True)  51.6 us
    dot_general x4, matrix products, contract_cols(): lax.dot_general(left, right, (((1,), (0,)), ((), ())), preferred_element_...  32.7 us
    dot_general x4, matrix products, contract_rows(): lax.dot_general(left, right, (((1,), (1,)), ((), ())), preferred_element_...  30.5 us
    ppermute x2, waiting for transfers between devices, branch(): lax.ppermute(current, 'blk', [(i, i ^ apart) for i in range(width)])  26.2 us
    all_to_all x1, starting transfers between devices, on_device(): lax.all_to_all(chunks.reshape(devices, capacity, width), ('dp', 'blk'), s...  18 us
    all_to_all x1, waiting for transfers between devices, on_device(): lax.all_to_all(chunks.reshape(devices, capacity, width), ('dp', 'blk'), s...  16.9 us
    gather x1, local copies, waits for them, and re-layouts, on_device(): energy = returned.reshape(slot_count)[position]  10.5 us
    unnamed x32, local copies, waits for them, and re-layouts  10.2 us
  transfers between devices with their start and end apart: 5, of which 3 were waited for; matrix products, arithmetic and copies ran while one was open for 28% of the time, Pallas kernels for 0%

commit v1 on v0

v1 whole, which is shorter than its diff:
```python
import functools
import math

import jax
import jax.numpy as jnp
from jax import lax
from jax.experimental import pallas as pl
from jax.experimental.pallas import tpu as pltpu
from jax.sharding import PartitionSpec as P

PASSES = 2
KAPPA = 64.0
ABSENT = 1.25
LIMIT = 1.125
EPS = 1e-06
FLAG_ROWS = 16
VMEM = pltpu.VMEM
F32 = jnp.float32
BF16 = jnp.bfloat16


def unit_vectors(values):
    wide = values.astype(F32)
    scale = lax.rsqrt(jnp.mean(wide * wide, axis=-1, keepdims=True) + EPS) * values.shape[-1] ** (
        -0.5
    )
    return (wide * scale).astype(BF16)


def iota(shape, axis):
    return lax.broadcasted_iota(jnp.int32, shape, axis)


def dot(left, right, dims, precision=None):
    return lax.dot_general(
        left, right, (dims, ((), ())), preferred_element_type=F32, precision=precision
    )


def pack_kernel(
    capacity, pair_ref, ids_ref, rows_ref, out_ref, marks_ref, place_ref, unit_ref, spot_ref, y_ref
):
    g = pl.program_id(0)
    rows = rows_ref.shape[0]
    devices = marks_ref.shape[0]
    slots = y_ref.shape[0]
    members = slots // capacity

    @pl.when(g == 0)
    def _():
        unit_ref[...] = unit_vectors(rows_ref[...])
        hot = jnp.where(ids_ref[...] == iota((rows, devices), 1), 1.0, 0.0)
        marks = hot.T
        marks_ref[...] = marks.astype(BF16)
        before = jnp.where(iota((rows, rows), 0) < iota((rows, rows), 1), 1.0, 0.0).astype(BF16)
        seen = dot(marks.astype(BF16), before, ((1,), (0,)))
        place = jnp.sum(seen * marks, axis=0, keepdims=True)
        owner = jnp.sum(iota((devices, rows), 0).astype(F32) * marks, axis=0, keepdims=True)
        place_ref[...] = place.astype(jnp.int32)
        spot_ref[...] = (owner * capacity + place).astype(jnp.int32)

    chosen = jnp.where(iota((slots, rows), 0) + g * slots == spot_ref[...], 1.0, 0.0)
    found = jnp.sum(chosen, axis=1, keepdims=True)
    y = dot(chosen.astype(BF16), unit_ref[...], ((1,), (0,)))
    mark = jnp.where(iota((slots, 128), 1) == 0, ABSENT, 0.0) * (1.0 - found)
    y_ref[...] = y.astype(BF16)
    y_ref[:, :128] = (y[:, :128] + mark).astype(BF16)
    for k in range(members):
        out_ref[0, k, 0] = y_ref[k * capacity : (k + 1) * capacity, :]
        for p in range(PASSES):
            start = pl.multiple_of(jnp.bitwise_xor(pair_ref[p], k) * capacity, capacity)
            out_ref[0, k, 1 + p] = y_ref[pl.ds(start, capacity), :]


def pack(rows, block_ids, pairing, groups, members, capacity):
    count, width = rows.shape
    devices = groups * members
    return pl.pallas_call(
        functools.partial(pack_kernel, capacity),
        grid=(groups,),
        in_specs=[
            pl.BlockSpec(memory_space=pltpu.SMEM),
            pl.BlockSpec((count, 1), lambda g: (0, 0)),
            pl.BlockSpec((count, width), lambda g: (0, 0)),
        ],
        out_specs=[
            pl.BlockSpec(
                (1, members, 1 + PASSES, capacity, width), lambda g: (g, 0, 0, 0, 0)
            ),
            pl.BlockSpec((devices, count), lambda g: (0, 0)),
            pl.BlockSpec((1, count), lambda g: (0, 0)),
        ],
        out_shape=[
            jax.ShapeDtypeStruct((groups, members, 1 + PASSES, capacity, width), BF16),
            jax.ShapeDtypeStruct((devices, count), BF16),
            jax.ShapeDtypeStruct((1, count), jnp.int32),
        ],
        scratch_shapes=[
            VMEM((count, width), BF16),
            VMEM((1, count), jnp.int32),
            VMEM((members * capacity, width), BF16),
        ],
        cost_estimate=pl.CostEstimate(
            flops=4 * count * count * width, bytes_accessed=20 << 20, transcendentals=0
        ),
        name="pack",
    )(pairing, block_ids, rows)


def affinity_kernel(tiles_ref, x_ref, aff_ref, total_ref, flag_ref, wide_ref):
    tile_rows, width = tiles_ref.shape

    @pl.when((pl.program_id(0) == 0) & (pl.program_id(1) == 0))
    def _():
        wide_ref[:tile_rows] = tiles_ref[...]
        wide_ref[tile_rows:] = jnp.where(
            iota((FLAG_ROWS, width), 1) == 0, 1.0, 0.0
        ).astype(BF16)

    x = x_ref[...].reshape(-1, width)
    scores = dot(wide_ref[...], x, ((1,), (1,)))
    aff = jnp.exp(KAPPA * scores[:tile_rows])
    total_ref[0] = jnp.sum(aff, axis=0, keepdims=True)
    flag_ref[0] = scores[tile_rows : tile_rows + 1]
    aff_ref[0] = aff.astype(BF16)


def affinity(tiles, got, p, block):
    tile_rows, width = tiles.shape
    sources, _, capacity, _ = got.shape
    slots = sources * capacity
    steps = slots // block
    return pl.pallas_call(
        affinity_kernel,
        grid=(2, steps),
        in_specs=[
            pl.BlockSpec((tile_rows, width), lambda c, i: (0, 0)),
            pl.BlockSpec(
                (block // capacity, 1, capacity, width), lambda c, i: (i, c * (1 + p), 0, 0)
            ),
        ],
        out_specs=[
            pl.BlockSpec((1, tile_rows, block), lambda c, i: (c, 0, i)),
            pl.BlockSpec((1, 1, block), lambda c, i: (c, 0, i)),
            pl.BlockSpec((1, 1, block), lambda c, i: (c, 0, i)),
        ],
        out_shape=[
            jax.ShapeDtypeStruct((2, tile_rows, slots), BF16),
            jax.ShapeDtypeStruct((2, 1, slots), F32),
            jax.ShapeDtypeStruct((2, 1, slots), F32),
        ],
        scratch_shapes=[VMEM((tile_rows + FLAG_ROWS, width), BF16)],
        cost_estimate=pl.CostEstimate(
            flops=4 * slots * tile_rows * width,
            bytes_accessed=16 << 20,
            transcendentals=2 * slots * tile_rows,
        ),
        name="affinity",
    )(tiles, got)


def sums_kernel(
    last, tiles_ref, aff_ref, x_ref, total_ref, swapped_ref, flag_ref, out_ref, acc_ref, count_ref
):
    c, i = pl.program_id(0), pl.program_id(1)
    tile_rows, width = tiles_ref.shape
    block = aff_ref.shape[2]

    @pl.when((c == 0) & (i == 0))
    def _():
        acc_ref[...] = jnp.zeros_like(acc_ref)
        count_ref[...] = jnp.zeros_like(count_ref)

    total = total_ref[0] + swapped_ref[0]
    inverse = jnp.where(flag_ref[0] < LIMIT, 1.0 / total, 0.0)
    weights = aff_ref[0].astype(F32) * inverse
    part = weights[:, :128]
    for n in range(1, block // 128):
        part = part + weights[:, n * 128 : (n + 1) * 128]
    count_ref[...] += part
    acc_ref[...] += dot(weights.astype(BF16), x_ref[...].reshape(-1, width), ((1,), (0,)))

    @pl.when((c == pl.num_programs(0) - 1) & (i == pl.num_programs(1) - 1))
    def _():
        counts = jnp.sum(count_ref[...], axis=1, keepdims=True)
        centers = (
            math.sqrt(width) * (acc_ref[...] + tiles_ref[...].astype(F32)) / (counts + 1.0)
        )
        out_ref[...] = centers if last else unit_vectors(centers)


def sums(tiles, aff, got, total, swapped, flag, p, block):
    tile_rows, width = tiles.shape
    sources, _, capacity, _ = got.shape
    slots = sources * capacity
    last = p == PASSES - 1
    row_spec = pl.BlockSpec((1, 1, block), lambda c, i: (c, 0, i))
    return pl.pallas_call(
        functools.partial(sums_kernel, last),
        grid=(2, slots // block),
        in_specs=[
            pl.BlockSpec((tile_rows, width), lambda c, i: (0, 0)),
            pl.BlockSpec((1, tile_rows, block), lambda c, i: (c, 0, i)),
            pl.BlockSpec(
                (block // capacity, 1, capacity, width), lambda c, i: (i, c * (1 + p), 0, 0)
            ),
            row_spec,
            pl.BlockSpec((1, 1, block), lambda c, i: (1 - c, 0, i)),
            row_spec,
        ],
        out_specs=pl.BlockSpec((tile_rows, width), lambda c, i: (0, 0)),
        out_shape=jax.ShapeDtypeStruct((tile_rows, width), F32 if last else BF16),
        scratch_shapes=[VMEM((tile_rows, width), F32), VMEM((tile_rows, 128), F32)],
        cost_estimate=pl.CostEstimate(
            flops=4 * slots * tile_rows * width, bytes_accessed=16 << 20, transcendentals=0
        ),
        name="sums",
    )(tiles, aff, got, total, swapped, flag)


def spread_kernel(capacity, total_ref, swapped_ref, out_ref):
    sources, lanes = out_ref.shape
    slots = total_ref.shape[2]
    total = total_ref[0] + swapped_ref[1]
    picked = jnp.where(
        iota((sources, slots), 1) // capacity == iota((sources, slots), 0), total, 0.0
    )
    place = jnp.where(
        iota((slots, lanes), 0) % capacity == iota((slots, lanes), 1), 1.0, 0.0
    )
    out_ref[...] = dot(picked, place, ((1,), (0,)), lax.Precision.HIGHEST)


def spread(total, swapped, sources, capacity):
    return pl.pallas_call(
        functools.partial(spread_kernel, capacity),
        out_shape=jax.ShapeDtypeStruct((sources, 128), F32),
        name="spread",
    )(total, swapped)


def energy_kernel(capacity, columns, back_ref, marks_ref, place_ref, out_ref):
    back = back_ref[...].T[:capacity]
    found = dot(back, marks_ref[...].astype(F32), ((1,), (0,)), lax.Precision.HIGHEST)
    mine = jnp.where(iota(found.shape, 0) == place_ref[...], found, 0.0)
    total = jnp.sum(mine, axis=0, keepdims=True)
    out_ref[...] = jnp.log(total / columns)


def energies(back, marks, place, capacity, columns):
    return pl.pallas_call(
        functools.partial(energy_kernel, capacity, columns),
        out_shape=jax.ShapeDtypeStruct(place.shape, F32),
        name="energies",
    )(back, marks, place)


def partner_swap(value, mask, width):
    def branch(apart):
        if apart == 0:
            return lambda current: current
        return lambda current: lax.ppermute(current, "blk", [(i, i ^ apart) for i in range(width)])

    return lax.switch(mask, [branch(apart) for apart in range(width)], value)


def on_device(rows, block_ids, centroids, pairing):
    groups = lax.axis_size("dp")
    members = lax.axis_size("blk")
    devices = groups * members
    rows_dev, width = rows.shape
    tile_rows = centroids.shape[0]
    capacity = 2 * rows_dev // devices
    sent, marks, place = pack(rows, block_ids, pairing, groups, members, capacity)
    got = lax.all_to_all(
        sent.reshape(devices, (1 + PASSES) * capacity, width),
        ("dp", "blk"),
        split_axis=0,
        concat_axis=0,
        tiled=True,
    ).reshape(devices, 1 + PASSES, capacity, width)
    tiles = unit_vectors(centroids)
    for p in range(PASSES):
        aff, total, flag = affinity(tiles, got, p, 512)
        swapped = partner_swap(total, pairing[p], members)
        if p == PASSES - 1:
            back = lax.all_to_all(
                spread(total, swapped, devices, capacity),
                ("dp", "blk"),
                split_axis=0,
                concat_axis=0,
                tiled=True,
            )
        tiles = sums(tiles, aff, got, total, swapped, flag, p, 512)
    energy = energies(back, marks, place, capacity, 2.0 * tile_rows)
    return (tiles, energy.reshape(rows_dev))


def solution(mesh):
    in_specs = (P(("dp", "blk"), None), P(("dp", "blk"), None), P(("dp", "blk"), None), P())
    out_specs = (P(("dp", "blk"), None), P(("dp", "blk")))
    return jax.shard_map(
        on_device, mesh=mesh, in_specs=in_specs, out_specs=out_specs, check_vma=False
    )
```

time: 271 us -> 223 us (0.82)
  waiting for transfers between devices: 43.2 us -> 116 us
  Pallas kernels: 0 us -> 69.2 us
  matrix products: 63.2 us -> 0 us
  blocking collectives: 51.6 us -> 0 us
  other arithmetic: 34.6 us -> 1.67 us
  local copies, waits for them, and re-layouts: 34.9 us -> 2.91 us
  starting transfers between devices: 39.4 us -> 29.9 us
    all_to_all x3 -> x2, waiting for transfers between devices: 17 us -> 110 us  [the longest x1 110 us: on_device(): lax.all_to_all(sent.reshape(devices, (1 + PASSES) * capacity, width), ('d...]
    pallas_call x0 -> x7, Pallas kernels: none -> 69.2 us  [the longest x2 28.3 us: sums(): pl.pallas_call(functools.partial(sums_kernel, last), grid=(2, slots // bl...]
    dot_general x8 -> x0, matrix products: 63.2 us -> none  [the longest x4 32.7 us: contract_cols(): lax.dot_general(left, right, (((1,), (0,)), ((), ())), preferred_element_...]
    all_to_all x1 -> x0, blocking collectives: 51.6 us -> none  [routed(): lax.all_to_all(sent, ('dp', 'blk'), split_axis=0, concat_axis=0, tiled=True)]
    ppermute x2, waiting for transfers between devices: 26.2 us -> 5.92 us  [branch(): lax.ppermute(current, 'blk', [(i, i ^ apart) for i in range(width)])]
    gather x3 -> x0, local copies, waits for them, and re-layouts: 17.5 us -> none  [the longest x1 10.5 us: on_device(): energy = returned.reshape(slot_count)[position]]
    reduce_sum x6 -> x1, other arithmetic: 15 us -> 0.27 us  [unit_vectors(): jnp.mean(wide * wide, axis=-1, keepdims=True) + EPS]
    all_to_all x3 -> x2, starting transfers between devices: 33.4 us -> 22.9 us  [the longest x1 11.9 us: on_device(): lax.all_to_all(sent.reshape(devices, (1 + PASSES) * capacity, width), ('d...]
  transfers between devices with their start and end apart: 5 -> 4, of which waited for: 3 -> 3; matrix products, arithmetic and copies ran while one was open for 28% -> 1% of each run, Pallas kernels for 0% -> 6%
where the time goes in v1:
time: 223 us; the launch traced here: 221 us
  waiting for transfers between devices  116 us (52%)
  Pallas kernels  69.2 us (31%)
  starting transfers between devices  29.9 us (13%)
  local copies, waits for them, and re-layouts  2.91 us (1%)
    all_to_all x1, waiting for transfers between devices, on_device(): lax.all_to_all(sent.reshape(devices, (1 + PASSES) * capacity, width), ('d...  110 us
    pallas_call x2, Pallas kernels, sums(): pl.pallas_call(functools.partial(sums_kernel, last), grid=(2, slots // bl...  28.3 us
    pallas_call x2, Pallas kernels, affinity(): pl.pallas_call(affinity_kernel, grid=(2, steps), in_specs=[pl.BlockSpec((...  26 us
    all_to_all x1, starting transfers between devices, on_device(): lax.all_to_all(sent.reshape(devices, (1 + PASSES) * capacity, width), ('d...  11.9 us
    all_to_all x1, starting transfers between devices, on_device(): lax.all_to_all(spread(total, swapped, devices, capacity), ('dp', 'blk'),...  11.1 us
    pallas_call x1, Pallas kernels, pack(): pl.pallas_call(functools.partial(pack_kernel, capacity), grid=(groups,),...  10.6 us
    ppermute x2, starting transfers between devices, branch(): lax.ppermute(current, 'blk', [(i, i ^ apart) for i in range(width)])  6.96 us
    ppermute x2, waiting for transfers between devices, branch(): lax.ppermute(current, 'blk', [(i, i ^ apart) for i in range(width)])  5.92 us
  transfers between devices with their start and end apart: 4, of which 3 were waited for; matrix products, arithmetic and copies ran while one was open for 1% of the time, Pallas kernels for 6%

profile of v1, /device:TPU:1, one launch (start us, length us, event | category | flops | bytes accessed | tf_op | source)
XLA Modules:
  0.0 221.3 jit_solution(17175575639921737128)
XLA Ops:
  0.6 1.7 copy.7.ids_ref
  2.3 10.6 %pack.1 = (bf16[8,16,3,16,768]{4,3,2,1,0:T(8,128)(2,1)}, bf16[128,1024]{1,0:T(8,128)(2,1)}, s32[1,1024]{1,0:T(1,128)}) custom-call(s32[2]{0:T(128)} %pair_ref.1, s32[1024,1]{1,0:T(8,128)} %copy.7.ids_ref, bf16[1024,768]{1,0:T(8,128)(2,1)} %rows_ref.1), custom_call_target="tpu_custom_call" | custom-call | flops 3221225472 | bytes 20971520 | tf_op jit(solution)/shard_map/pack/pallas_call | solution.py:78
  13.0 0.0 copy-start.2
  13.0 0.0 copy-start
  13.0 11.9 %all-to-all-start = ((bf16[128,48,768]{2,1,0:T(8,128)(2,1)}), bf16[128,48,768]{2,1,0:T(8,128)(2,1)}, u32[]{:S(2)}, u32[]{:S(2)}) async-start(bf16[128,48,768]{2,1,0:T(8,128)(2,1)} %bitcast.9), calls=%async_computation | async-start | bytes 18874368 | tf_op jit(solution)/shard_map/all_to_all | solution.py:275
  24.9 0.0 copy-done.2
  24.9 0.6 fusion
  26.8 0.0 copy-done
  26.8 0.3 multiply_reduce_fusion
  27.1 1.4 multiply_convert_fusion.tiles_ref
  28.4 109.7 %all-to-all-done = bf16[128,48,768]{2,1,0:T(8,128)(2,1)} async-done(((bf16[128,48,768]{2,1,0:T(8,128)(2,1)}), bf16[128,48,768]{2,1,0:T(8,128)(2,1)}, u32[]{:S(2)}, u32[]{:S(2)}) %all-to-all-start) | async-done | bytes 9437216 | tf_op jit(solution)/shard_map/all_to_all | solution.py:275
  138.1 13.0 %affinity.2 = (bf16[2,1024,2048]{2,1,0:T(8,128)(2,1)}, f32[2,1,2048]{2,1,0:T(1,128)S(1)}, f32[2,1,2048]{2,1,0:T(1,128)}) custom-call(bf16[1024,768]{1,0:T(8,128)(2,1)} %multiply_convert_fusion.tiles_ref, bf16[128,3,16,768]{3,2,1,0:T(8,128)(2,1)} %bitcast.1.x_ref), custom_call_target="tpu_custom_call" | custom-call | flops 6442450944 | bytes 16777216 | tf_op jit(solution)/shard_map/affinity/pallas_call | solution.py:133
  151.1 6.6 %conditional.2 = (f32[2,1,2048]{2,1,0:T(1,128)}) conditional(s32[]{:T(128)} %bitcast.2, f32[2,1,2048]{2,1,0:T(1,128)S(1)} %get-tuple-element.79.total_ref, f32[2,1,2048]{2,1,0:T(1,128)S(1)} %get-tuple-element.79.total_ref, f32[2,1,2048]{2,1,0:T(1,128)S(1)} %get-tuple-element.79.total_ref, ...), branch_computations={%region_1.0_spmd, %region_2.0_spmd, %region_3.0_spmd, %region_4.0_... | conditional | bytes 65584 | solution.py:264
  151.1 5.3 %collective-permute-start.1 = (f32[2,1,2048]{2,1,0:T(1,128)S(1)}, f32[2,1,2048]{2,1,0:T(1,128)}, u32[]{:S(2)}, u32[]{:S(2)}) collective-permute-start(f32[2,1,2048]{2,1,0:T(1,128)S(1)} %param.2), channel_id=1, source_target_pairs={{0,2},{1,3},{2,0},{3,1},{4,6},{5,7},{6,4},{7,5},{8,10},{9,11},{10,... | collective-permute-start | bytes 49160 | tf_op jit(solution)/shard_map/cond/branch_2_fun/ppermute | solution.py:262
  156.5 1.2 collective-permute-done.1
  157.7 14.1 %sums.2.tiles_ref = bf16[1024,768]{1,0:T(8,128)(2,1)} custom-call(bf16[1024,768]{1,0:T(8,128)(2,1)} %multiply_convert_fusion.tiles_ref, bf16[2,1024,2048]{2,1,0:T(8,128)(2,1)} %get-tuple-element.78.aff_ref, bf16[128,3,16,768]{3,2,1,0:T(8,128)(2,1)} %bitcast.1.x_ref, f32[2,1,2048]{2,1,0:T(1,128)S(1)} %get-tuple-element.79.total_ref, ...), custom_call_target="tpu_custom_call" | custom-call | flops 6442450944 | bytes 16777216 | tf_op jit(solution)/shard_map/sums/pallas_call | solution.py:198
  171.8 13.0 %affinity.3 = (bf16[2,1024,2048]{2,1,0:T(8,128)(2,1)}, f32[2,1,2048]{2,1,0:T(1,128)S(1)}, f32[2,1,2048]{2,1,0:T(1,128)}) custom-call(bf16[1024,768]{1,0:T(8,128)(2,1)} %sums.2.tiles_ref, bf16[128,3,16,768]{3,2,1,0:T(8,128)(2,1)} %bitcast.1.x_ref), custom_call_target="tpu_custom_call" | custom-call | flops 6442450944 | bytes 16777216 | tf_op jit(solution)/shard_map/affinity/pallas_call | solution.py:133
  184.8 6.3 %conditional.3 = (f32[2,1,2048]{2,1,0:T(1,128)}) conditional(s32[]{:T(128)} %bitcast.3, f32[2,1,2048]{2,1,0:T(1,128)S(1)} %get-tuple-element.82.total_ref, f32[2,1,2048]{2,1,0:T(1,128)S(1)} %get-tuple-element.82.total_ref, f32[2,1,2048]{2,1,0:T(1,128)S(1)} %get-tuple-element.82.total_ref, ...), branch_computations={%region_17.0_spmd, %region_18.0_spmd, %region_19.0_spmd, %region_2... | conditional | bytes 65584 | solution.py:264
  184.8 1.6 collective-permute-start.28
  186.4 4.7 %collective-permute-done.28 = f32[2,1,2048]{2,1,0:T(1,128)} collective-permute-done((f32[2,1,2048]{2,1,0:T(1,128)S(1)}, f32[2,1,2048]{2,1,0:T(1,128)}, u32[]{:S(2)}, u32[]{:S(2)}) %collective-permute-start.28) | collective-permute-done | bytes 16416 | tf_op jit(solution)/shard_map/cond/branch_14_fun/ppermute | solution.py:262
  191.1 2.4 %spread.1 = f32[128,128]{1,0:T(8,128)} custom-call(f32[2,1,2048]{2,1,0:T(1,128)S(1)} %get-tuple-element.82.total_ref, f32[2,1,2048]{2,1,0:T(1,128)} %get-tuple-element.89.swapped_ref), custom_call_target="tpu_custom_call" | custom-call | tf_op jit(solution)/shard_map/spread/pallas_call | solution.py:235
  193.4 11.1 %all-to-all-start.1 = ((f32[128,1,128]{2,1,0:T(1,128)}), f32[128,1,128]{2,1,0:T(1,128)S(1)}, u32[]{:S(2)}, u32[]{:S(2)}) async-start(f32[128,1,128]{2,1,0:T(1,128)} %bitcast.10), calls=%async_computation.1 | async-start | bytes 131072 | tf_op jit(solution)/shard_map/all_to_all | solution.py:287
  204.5 14.2 %sums.3 = f32[1024,768]{1,0:T(8,128)} custom-call(bf16[1024,768]{1,0:T(8,128)(2,1)} %sums.2.tiles_ref, bf16[2,1024,2048]{2,1,0:T(8,128)(2,1)} %get-tuple-element.81.aff_ref, bf16[128,3,16,768]{3,2,1,0:T(8,128)(2,1)} %bitcast.1.x_ref, f32[2,1,2048]{2,1,0:T(1,128)S(1)} %get-tuple-element.82.total_ref, f32[2,1,2048]{2,1,0:T(1,128)} %get-tuple-element.89.swapped_ref, ...), custom_call_target="tpu_custom_call" | custom-call | flops 6442450944 | bytes 16777216 | tf_op jit(solution)/shard_map/sums/pallas_call | solution.py:198
  218.7 0.0 all-to-all-done.1
  218.7 0.0 copy-start.1
  218.7 0.6 copy-done.1
  219.3 1.9 energies.1
  (1 shorter events, 0.0 us)
Async XLA Ops:
  13.0 11.9 %copy-start.2 = (s32[2]{0:T(128)S(1)}, s32[2]{0:T(128)}, u32[]{:S(2)}) copy-start(s32[2]{0:T(128)} %pair_ref.1) | copy-start | bytes 28
  13.0 13.8 %copy-start = (f32[1024,768]{1,0:T(8,128)S(1)}, f32[1024,768]{1,0:T(8,128)}, u32[]{:S(2)}) copy-start(f32[1024,768]{1,0:T(8,128)} %param.38) | copy-start | bytes 9437188
  13.0 125.2 %all-to-all-start = ((bf16[128,48,768]{2,1,0:T(8,128)(2,1)}), bf16[128,48,768]{2,1,0:T(8,128)(2,1)}, u32[]{:S(2)}, u32[]{:S(2)}) async-start(bf16[128,48,768]{2,1,0:T(8,128)(2,1)} %bitcast.9), calls=%async_computation | async-start | bytes 18874368 | tf_op jit(solution)/shard_map/all_to_all | solution.py:275
  151.1 6.6 %collective-permute-start.1 = (f32[2,1,2048]{2,1,0:T(1,128)S(1)}, f32[2,1,2048]{2,1,0:T(1,128)}, u32[]{:S(2)}, u32[]{:S(2)}) collective-permute-start(f32[2,1,2048]{2,1,0:T(1,128)S(1)} %param.2), channel_id=1, source_target_pairs={{0,2},{1,3},{2,0},{3,1},{4,6},{5,7},{6,4},{7,5},{8,10},{9,11},{10,... | collective-permute-start | bytes 49160 | tf_op jit(solution)/shard_map/cond/branch_2_fun/ppermute | solution.py:262
  184.8 6.3 %collective-permute-start.28 = (f32[2,1,2048]{2,1,0:T(1,128)S(1)}, f32[2,1,2048]{2,1,0:T(1,128)}, u32[]{:S(2)}, u32[]{:S(2)}) collective-permute-start(f32[2,1,2048]{2,1,0:T(1,128)S(1)} %param.30), channel_id=1, source_target_pairs={{0,14},{1,15},{2,12},{3,13},{4,10},{5,11},{6,8},{7,9},{8,6},{9,7},... | collective-permute-start | bytes 49160 | tf_op jit(solution)/shard_map/cond/branch_14_fun/ppermute | solution.py:262
  193.4 25.3 %all-to-all-start.1 = ((f32[128,1,128]{2,1,0:T(1,128)}), f32[128,1,128]{2,1,0:T(1,128)S(1)}, u32[]{:S(2)}, u32[]{:S(2)}) async-start(f32[128,1,128]{2,1,0:T(1,128)} %bitcast.10), calls=%async_computation.1 | async-start | bytes 131072 | tf_op jit(solution)/shard_map/all_to_all | solution.py:287
  218.7 0.6 copy-start.1

commit v2 on v1

--- a/solution.py
+++ b/solution.py
@@ -44,20 +44,26 @@
     rows = rows_ref.shape[0]
     devices = marks_ref.shape[0]
     slots = y_ref.shape[0]
-    members = slots // capacity
+    groups, members = out_ref.shape[:2]
 
     @pl.when(g == 0)
     def _():
         unit_ref[...] = unit_vectors(rows_ref[...])
-        hot = jnp.where(ids_ref[...] == iota((rows, devices), 1), 1.0, 0.0)
-        marks = hot.T
+        marks = jnp.where(ids_ref[...] == iota((devices, rows), 0), 1.0, 0.0)
         marks_ref[...] = marks.astype(BF16)
-        before = jnp.where(iota((rows, rows), 0) < iota((rows, rows), 1), 1.0, 0.0).astype(BF16)
-        seen = dot(marks.astype(BF16), before, ((1,), (0,)))
-        place = jnp.sum(seen * marks, axis=0, keepdims=True)
-        owner = jnp.sum(iota((devices, rows), 0).astype(F32) * marks, axis=0, keepdims=True)
-        place_ref[...] = place.astype(jnp.int32)
-        spot_ref[...] = (owner * capacity + place).astype(jnp.int32)
+        pieces = [marks[:, n : n + 128] for n in range(0, rows, 128)]
+        before = jnp.where(iota((128, 128), 0) < iota((128, 128), 1), 1.0, 0.0).astype(BF16)
+        seen = dot(jnp.concatenate(pieces, axis=0).astype(BF16), before, ((1,), (0,)))
+        whose = iota((devices, 128), 0).astype(F32)
+        passed = jnp.zeros((devices, 1), F32)
+        for n, piece in enumerate(pieces):
+            lanes = slice(n * 128, (n + 1) * 128)
+            here = seen[n * devices : (n + 1) * devices] + passed
+            place = jnp.sum(here * piece, axis=0, keepdims=True)
+            owner = jnp.sum(whose * piece, axis=0, keepdims=True)
+            place_ref[:, lanes] = place.astype(jnp.int32)
+            spot_ref[:, lanes] = (owner * capacity + place).astype(jnp.int32)
+            passed = passed + jnp.sum(piece, axis=1, keepdims=True)
 
     chosen = jnp.where(iota((slots, rows), 0) + g * slots == spot_ref[...], 1.0, 0.0)
     found = jnp.sum(chosen, axis=1, keepdims=True)
@@ -65,27 +71,30 @@
     mark = jnp.where(iota((slots, 128), 1) == 0, ABSENT, 0.0) * (1.0 - found)
     y_ref[...] = y.astype(BF16)
     y_ref[:, :128] = (y[:, :128] + mark).astype(BF16)
-    for k in range(members):
-        out_ref[0, k, 0] = y_ref[k * capacity : (k + 1) * capacity, :]
-        for p in range(PASSES):
-            start = pl.multiple_of(jnp.bitwise_xor(pair_ref[p], k) * capacity, capacity)
-            out_ref[0, k, 1 + p] = y_ref[pl.ds(start, capacity), :]
-
-
-def pack(rows, block_ids, pairing, groups, members, capacity):
+    for h in range(groups):
+        base = h * members * capacity
+        for k in range(members):
+            out_ref[h, k, 0] = y_ref[base + k * capacity : base + (k + 1) * capacity, :]
+            for p in range(PASSES):
+                start = base + jnp.bitwise_xor(pair_ref[p], k) * capacity
+                out_ref[h, k, 1 + p] = y_ref[pl.ds(pl.multiple_of(start, capacity), capacity), :]
+
+
+def pack(rows, block_ids, pairing, groups, members, capacity, steps):
     count, width = rows.shape
     devices = groups * members
     return pl.pallas_call(
         functools.partial(pack_kernel, capacity),
-        grid=(groups,),
+        grid=(steps,),
         in_specs=[
             pl.BlockSpec(memory_space=pltpu.SMEM),
-            pl.BlockSpec((count, 1), lambda g: (0, 0)),
+            pl.BlockSpec((1, count), lambda g: (0, 0)),
             pl.BlockSpec((count, width), lambda g: (0, 0)),
         ],
         out_specs=[
             pl.BlockSpec(
-                (1, members, 1 + PASSES, capacity, width), lambda g: (g, 0, 0, 0, 0)
+                (groups // steps, members, 1 + PASSES, capacity, width),
+                lambda g: (g, 0, 0, 0, 0),
             ),
             pl.BlockSpec((devices, count), lambda g: (0, 0)),
             pl.BlockSpec((1, count), lambda g: (0, 0)),
@@ -98,17 +107,20 @@
         scratch_shapes=[
             VMEM((count, width), BF16),
             VMEM((1, count), jnp.int32),
-            VMEM((members * capacity, width), BF16),
+            VMEM((devices * capacity // steps, width), BF16),
         ],
         cost_estimate=pl.CostEstimate(
             flops=4 * count * count * width, bytes_accessed=20 << 20, transcendentals=0
         ),
         name="pack",
-    )(pairing, block_ids, rows)
-
-
-def affinity_kernel(tiles_ref, x_ref, aff_ref, total_ref, flag_ref, wide_ref):
+    )(pairing, block_ids.reshape(1, count), rows)
+
+
+def affinity_kernel(last, inner, tiles_ref, x_ref, aff_ref, total_ref, flag_ref, *rest):
+    wide_ref = rest[-1]
     tile_rows, width = tiles_ref.shape
+    capacity = x_ref.shape[2]
+    block = aff_ref.shape[2]
 
     @pl.when((pl.program_id(0) == 0) & (pl.program_id(1) == 0))
     def _():
@@ -117,38 +129,47 @@
             iota((FLAG_ROWS, width), 1) == 0, 1.0, 0.0
         ).astype(BF16)
 
-    x = x_ref[...].reshape(-1, width)
-    scores = dot(wide_ref[...], x, ((1,), (1,)))
-    aff = jnp.exp(KAPPA * scores[:tile_rows])
-    total_ref[0] = jnp.sum(aff, axis=0, keepdims=True)
-    flag_ref[0] = scores[tile_rows : tile_rows + 1]
-    aff_ref[0] = aff.astype(BF16)
-
-
-def affinity(tiles, got, p, block):
+    count = inner // capacity
+    for n in range(block // inner):
+        lanes = slice(n * inner, (n + 1) * inner)
+        x = x_ref[n * count : (n + 1) * count].reshape(inner, width)
+        scores = dot(wide_ref[...], x, ((1,), (1,)))
+        aff = jnp.exp2((KAPPA * math.log2(math.e)) * scores[:tile_rows])
+        total = jnp.sum(aff, axis=0, keepdims=True)
+        total_ref[0, :, lanes] = total
+        flag_ref[0, :, lanes] = scores[tile_rows : tile_rows + 1]
+        aff_ref[0, :, lanes] = aff.astype(BF16)
+        if last:
+            for v in range(inner // 128):
+                piece = total[:, v * 128 : (v + 1) * 128]
+                for k in range(128 // capacity):
+                    source = (n * inner + v * 128) // capacity + k
+                    rest[0][source] = pltpu.roll(piece, (128 - k * capacity) % 128, 1)
+
+
+def affinity(tiles, got, p, block, inner):
     tile_rows, width = tiles.shape
     sources, _, capacity, _ = got.shape
     slots = sources * capacity
-    steps = slots // block
+    last = p == PASSES - 1
+    row_spec = pl.BlockSpec((1, 1, block), lambda c, i: (c, 0, i))
+    row_shape = jax.ShapeDtypeStruct((2, 1, slots), F32)
+    out_specs = [pl.BlockSpec((1, tile_rows, block), lambda c, i: (c, 0, i)), row_spec, row_spec]
+    out_shape = [jax.ShapeDtypeStruct((2, tile_rows, slots), BF16), row_shape, row_shape]
+    if last:
+        out_specs.append(pl.BlockSpec((block // capacity, 1, 128), lambda c, i: (i, 0, c)))
+        out_shape.append(jax.ShapeDtypeStruct((sources, 1, 256), F32))
     return pl.pallas_call(
-        affinity_kernel,
-        grid=(2, steps),
+        functools.partial(affinity_kernel, last, inner),
+        grid=(2, slots // block),
         in_specs=[
             pl.BlockSpec((tile_rows, width), lambda c, i: (0, 0)),
             pl.BlockSpec(
                 (block // capacity, 1, capacity, width), lambda c, i: (i, c * (1 + p), 0, 0)
             ),
         ],
-        out_specs=[
-            pl.BlockSpec((1, tile_rows, block), lambda c, i: (c, 0, i)),
-            pl.BlockSpec((1, 1, block), lambda c, i: (c, 0, i)),
-            pl.BlockSpec((1, 1, block), lambda c, i: (c, 0, i)),
-        ],
-        out_shape=[
-            jax.ShapeDtypeStruct((2, tile_rows, slots), BF16),
-            jax.ShapeDtypeStruct((2, 1, slots), F32),
-            jax.ShapeDtypeStruct((2, 1, slots), F32),
-        ],
+        out_specs=out_specs,
+        out_shape=out_shape,
         scratch_shapes=[VMEM((tile_rows + FLAG_ROWS, width), BF16)],
         cost_estimate=pl.CostEstimate(
             flops=4 * slots * tile_rows * width,
@@ -218,41 +239,33 @@
     )(tiles, aff, got, total, swapped, flag)
 
 
-def spread_kernel(capacity, total_ref, swapped_ref, out_ref):
-    sources, lanes = out_ref.shape
-    slots = total_ref.shape[2]
-    total = total_ref[0] + swapped_ref[1]
-    picked = jnp.where(
-        iota((sources, slots), 1) // capacity == iota((sources, slots), 0), total, 0.0
-    )
-    place = jnp.where(
-        iota((slots, lanes), 0) % capacity == iota((slots, lanes), 1), 1.0, 0.0
-    )
-    out_ref[...] = dot(picked, place, ((1,), (0,)), lax.Precision.HIGHEST)
-
-
-def spread(total, swapped, sources, capacity):
-    return pl.pallas_call(
-        functools.partial(spread_kernel, capacity),
-        out_shape=jax.ShapeDtypeStruct((sources, 128), F32),
-        name="spread",
-    )(total, swapped)
-
-
-def energy_kernel(capacity, columns, back_ref, marks_ref, place_ref, out_ref):
-    back = back_ref[...].T[:capacity]
-    found = dot(back, marks_ref[...].astype(F32), ((1,), (0,)), lax.Precision.HIGHEST)
+def energy_kernel(capacity, columns, pair_ref, back_ref, marks_ref, place_ref, out_ref):
+    devices = back_ref.shape[0]
+    across = jnp.where(
+        jnp.bitwise_xor(iota((devices, devices), 0), pair_ref[PASSES - 1])
+        == iota((devices, devices), 1),
+        1.0,
+        0.0,
+    )
+    total = back_ref[:, 0, :128] + dot(
+        across, back_ref[:, 0, 128:], ((1,), (0,)), lax.Precision.HIGHEST
+    )
+    found = dot(
+        total.T[:capacity], marks_ref[...].astype(F32), ((1,), (0,)), lax.Precision.HIGHEST
+    )
     mine = jnp.where(iota(found.shape, 0) == place_ref[...], found, 0.0)
-    total = jnp.sum(mine, axis=0, keepdims=True)
-    out_ref[...] = jnp.log(total / columns)
-
-
-def energies(back, marks, place, capacity, columns):
+    out_ref[...] = jnp.log(jnp.sum(mine, axis=0, keepdims=True) / columns)
+
+
+def energies(pairing, back, marks, place, capacity, columns):
+    whole = pl.BlockSpec(memory_space=VMEM)
     return pl.pallas_call(
         functools.partial(energy_kernel, capacity, columns),
+        in_specs=[pl.BlockSpec(memory_space=pltpu.SMEM), whole, whole, whole],
+        out_specs=whole,
         out_shape=jax.ShapeDtypeStruct(place.shape, F32),
         name="energies",
-    )(back, marks, place)
+    )(pairing, back, marks, place)
 
 
 def partner_swap(value, mask, width):
@@ -271,7 +284,7 @@
     rows_dev, width = rows.shape
     tile_rows = centroids.shape[0]
     capacity = 2 * rows_dev // devices
-    sent, marks, place = pack(rows, block_ids, pairing, groups, members, capacity)
+    sent, marks, place = pack(rows, block_ids, pairing, groups, members, capacity, 2)
     got = lax.all_to_all(
         sent.reshape(devices, (1 + PASSES) * capacity, width),
         ("dp", "blk"),
@@ -281,18 +294,14 @@
     ).reshape(devices, 1 + PASSES, capacity, width)
     tiles = unit_vectors(centroids)
     for p in range(PASSES):
-        aff, total, flag = affinity(tiles, got, p, 512)
+        aff, total, flag, *spread = affinity(tiles, got, p, 1024, 512)
+        if spread:
+            back = lax.all_to_all(
+                spread[0], ("dp", "blk"), split_axis=0, concat_axis=0, tiled=True
+            )
         swapped = partner_swap(total, pairing[p], members)
-        if p == PASSES - 1:
-            back = lax.all_to_all(
-                spread(total, swapped, devices, capacity),
-                ("dp", "blk"),
-                split_axis=0,
-                concat_axis=0,
-                tiled=True,
-            )
-        tiles = sums(tiles, aff, got, total, swapped, flag, p, 512)
-    energy = energies(back, marks, place, capacity, 2.0 * tile_rows)
+        tiles = sums(tiles, aff, got, total, swapped, flag, p, 1024)
+    energy = energies(pairing, back, marks, place, capacity, 2.0 * tile_rows)
     return (tiles, energy.reshape(rows_dev))
 
 

time: 223 us -> 206 us (0.924)
  Pallas kernels: 69.2 us -> 59.4 us
  starting transfers between devices: 29.9 us -> 27.1 us
    pallas_call x5 -> x4, Pallas kernels: 40.9 us -> 34.4 us  [the longest x2 22.6 us: affinity(): pl.pallas_call(functools.partial(affinity_kernel, last, inner), grid=(2,...]
    ppermute x2, starting transfers between devices: 6.96 us -> 2.99 us  [branch(): lax.ppermute(current, 'blk', [(i, i ^ apart) for i in range(width)])]
    pallas_call x2, Pallas kernels: 28.3 us -> 25 us  [sums(): pl.pallas_call(functools.partial(sums_kernel, last), grid=(2, slots // bl...]
where the time goes in v2:
time: 206 us
  waiting for transfers between devices  115 us (56%)
  Pallas kernels  59.4 us (29%)
  starting transfers between devices  27.1 us (13%)
    all_to_all x1, waiting for transfers between devices, on_device(): lax.all_to_all(sent.reshape(devices, (1 + PASSES) * capacity, width), ('d...  110 us
    pallas_call x2, Pallas kernels, sums(): pl.pallas_call(functools.partial(sums_kernel, last), grid=(2, slots // bl...  25 us
    pallas_call x2, Pallas kernels, affinity(): pl.pallas_call(functools.partial(affinity_kernel, last, inner), grid=(2,...  22.6 us
    all_to_all x1, starting transfers between devices, on_device(): lax.all_to_all(spread[0], ('dp', 'blk'), split_axis=0, concat_axis=0, til...  12.3 us
    all_to_all x1, starting transfers between devices, on_device(): lax.all_to_all(sent.reshape(devices, (1 + PASSES) * capacity, width), ('d...  11.9 us
    pallas_call x1, Pallas kernels, pack(): pl.pallas_call(functools.partial(pack_kernel, capacity), grid=(steps,), i...  9.61 us
    ppermute x2, waiting for transfers between devices, branch(): lax.ppermute(current, 'blk', [(i, i ^ apart) for i in range(width)])  5.16 us
  transfers between devices with their start and end apart: 4, of which 3 were waited for; matrix products, arithmetic and copies ran while one was open for 1% of the time, Pallas kernels for 6%

profile of v2, /device:TPU:1, one launch (start us, length us, event | category | flops | bytes accessed | tf_op | source)
XLA Modules:
  0.0 206.3 jit_solution(17738834255234847833)
XLA Ops:
  0.6 9.6 %pack.1 = (bf16[8,16,3,16,768]{4,3,2,1,0:T(8,128)(2,1)}, bf16[128,1024]{1,0:T(8,128)(2,1)}, s32[1,1024]{1,0:T(1,128)}) custom-call(s32[2]{0:T(128)} %pair_ref.3, s32[1,1024]{1,0:T(1,128)} %bitcast.8, bf16[1024,768]{1,0:T(8,128)(2,1)} %rows_ref.1), custom_call_target="tpu_custom_call" | custom-call | flops 3221225472 | bytes 20971520 | tf_op jit(solution)/shard_map/pack/pallas_call | solution.py:86
  10.2 0.0 copy-start.2
  10.2 0.0 copy-start
  10.2 11.9 %all-to-all-start = ((bf16[128,48,768]{2,1,0:T(8,128)(2,1)}), bf16[128,48,768]{2,1,0:T(8,128)(2,1)}, u32[]{:S(2)}, u32[]{:S(2)}) async-start(bf16[128,48,768]{2,1,0:T(8,128)(2,1)} %bitcast.6), calls=%async_computation | async-start | bytes 18874368 | tf_op jit(solution)/shard_map/all_to_all | solution.py:288
  22.1 0.0 copy-done.2
  22.1 0.6 fusion
  24.0 0.0 copy-done
  24.0 0.3 multiply_reduce_fusion
  24.3 1.4 multiply_convert_fusion.tiles_ref
  25.7 109.7 %all-to-all-done = bf16[128,48,768]{2,1,0:T(8,128)(2,1)} async-done(((bf16[128,48,768]{2,1,0:T(8,128)(2,1)}), bf16[128,48,768]{2,1,0:T(8,128)(2,1)}, u32[]{:S(2)}, u32[]{:S(2)}) %all-to-all-start) | async-done | bytes 9437216 | tf_op jit(solution)/shard_map/all_to_all | solution.py:288
  135.4 11.2 %affinity.2 = (bf16[2,1024,2048]{2,1,0:T(8,128)(2,1)}, f32[2,1,2048]{2,1,0:T(1,128)S(1)}, f32[2,1,2048]{2,1,0:T(1,128)}) custom-call(bf16[1024,768]{1,0:T(8,128)(2,1)} %multiply_convert_fusion.tiles_ref, bf16[128,3,16,768]{3,2,1,0:T(8,128)(2,1)} %bitcast.2.x_ref), custom_call_target="tpu_custom_call" | custom-call | flops 6442450944 | bytes 16777216 | tf_op jit(solution)/shard_map/affinity/pallas_call | solution.py:162
  146.6 3.6 %conditional.2 = (f32[2,1,2048]{2,1,0:T(1,128)}) conditional(s32[]{:T(128)} %bitcast.3, f32[2,1,2048]{2,1,0:T(1,128)S(1)} %get-tuple-element.80.total_ref, f32[2,1,2048]{2,1,0:T(1,128)S(1)} %get-tuple-element.80.total_ref, f32[2,1,2048]{2,1,0:T(1,128)S(1)} %get-tuple-element.80.total_ref, ...), branch_computations={%region_1.0_spmd, %region_2.0_spmd, %region_3.0_spmd, %region_4.0_... | conditional | bytes 65584 | solution.py:277
  146.6 0.0 collective-permute-start.4
  146.7 3.5 %collective-permute-done.4 = f32[2,1,2048]{2,1,0:T(1,128)} collective-permute-done((f32[2,1,2048]{2,1,0:T(1,128)S(1)}, f32[2,1,2048]{2,1,0:T(1,128)}, u32[]{:S(2)}, u32[]{:S(2)}) %collective-permute-start.4) | collective-permute-done | bytes 16416 | tf_op jit(solution)/shard_map/cond/branch_5_fun/ppermute | solution.py:275
  150.2 12.4 %sums.2.tiles_ref = bf16[1024,768]{1,0:T(8,128)(2,1)} custom-call(bf16[1024,768]{1,0:T(8,128)(2,1)} %multiply_convert_fusion.tiles_ref, bf16[2,1024,2048]{2,1,0:T(8,128)(2,1)} %get-tuple-element.79.aff_ref, bf16[128,3,16,768]{3,2,1,0:T(8,128)(2,1)} %bitcast.2.x_ref, f32[2,1,2048]{2,1,0:T(1,128)S(1)} %get-tuple-element.80.total_ref, ...), custom_call_target="tpu_custom_call" | custom-call | flops 6442450944 | bytes 16777216 | tf_op jit(solution)/shard_map/sums/pallas_call | solution.py:219
  162.7 11.4 %affinity.3 = (bf16[2,1024,2048]{2,1,0:T(8,128)(2,1)}, f32[2,1,2048]{2,1,0:T(1,128)S(1)}, f32[2,1,2048]{2,1,0:T(1,128)}, f32[128,1,256]{2,1,0:T(1,128)}) custom-call(bf16[1024,768]{1,0:T(8,128)(2,1)} %sums.2.tiles_ref, bf16[128,3,16,768]{3,2,1,0:T(8,128)(2,1)} %bitcast.2.x_ref), custom_call_target="tpu_custom_call" | custom-call | flops 6442450944 | bytes 16777216 | tf_op jit(solution)/shard_map/affinity/pallas_call | solution.py:162
  174.0 12.3 %all-to-all-start.1 = ((f32[128,1,256]{2,1,0:T(1,128)}), f32[128,1,256]{2,1,0:T(1,128)S(1)}, u32[]{:S(2)}, u32[]{:S(2)}) async-start(f32[128,1,256]{2,1,0:T(1,128)} %get-tuple-element.85), calls=%async_computation.1 | async-start | bytes 262144 | tf_op jit(solution)/shard_map/all_to_all | solution.py:299
  186.3 4.6 %conditional.3 = (f32[2,1,2048]{2,1,0:T(1,128)}) conditional(s32[]{:T(128)} %bitcast.4, f32[2,1,2048]{2,1,0:T(1,128)S(1)} %get-tuple-element.83.total_ref, f32[2,1,2048]{2,1,0:T(1,128)S(1)} %get-tuple-element.83.total_ref, f32[2,1,2048]{2,1,0:T(1,128)S(1)} %get-tuple-element.83.total_ref, ...), branch_computations={%region_17.0_spmd, %region_18.0_spmd, %region_19.0_spmd, %region_2... | conditional | bytes 65584 | solution.py:277
  186.3 2.9 %collective-permute-start.16 = (f32[2,1,2048]{2,1,0:T(1,128)S(1)}, f32[2,1,2048]{2,1,0:T(1,128)}, u32[]{:S(2)}, u32[]{:S(2)}) collective-permute-start(f32[2,1,2048]{2,1,0:T(1,128)S(1)} %param.18), channel_id=1, source_target_pairs={{0,2},{1,3},{2,0},{3,1},{4,6},{5,7},{6,4},{7,5},{8,10},{9,11},{10,... | collective-permute-start | bytes 49160 | tf_op jit(solution)/shard_map/cond/branch_2_fun/ppermute | solution.py:275
  189.3 1.6 collective-permute-done.16
  190.9 12.5 %sums.3 = f32[1024,768]{1,0:T(8,128)} custom-call(bf16[1024,768]{1,0:T(8,128)(2,1)} %sums.2.tiles_ref, bf16[2,1024,2048]{2,1,0:T(8,128)(2,1)} %get-tuple-element.82.aff_ref, bf16[128,3,16,768]{3,2,1,0:T(8,128)(2,1)} %bitcast.2.x_ref, f32[2,1,2048]{2,1,0:T(1,128)S(1)} %get-tuple-element.83.total_ref, f32[2,1,2048]{2,1,0:T(1,128)} %get-tuple-element.91.swapped_ref, ...), custom_call_target="tpu_custom_call" | custom-call | flops 6442450944 | bytes 16777216 | tf_op jit(solution)/shard_map/sums/pallas_call | solution.py:219
  203.4 0.0 all-to-all-done.1.back_ref
  203.5 0.0 copy-start.1
  203.5 0.6 copy-done.1
  204.1 2.2 %energies.1 = f32[1,1024]{1,0:T(1,128)} custom-call(s32[2]{0:T(128)} %pair_ref.3, f32[128,1,256]{2,1,0:T(1,128)} %copy-done.1, bf16[128,1024]{1,0:T(8,128)(2,1)} %get-tuple-element.86.marks_ref, s32[1,1024]{1,0:T(1,128)} %get-tuple-element.87.place_ref), custom_call_target="tpu_custom_call" | custom-call | tf_op jit(solution)/shard_map/energies/pallas_call | solution.py:262
  (1 shorter events, 0.0 us)
Async XLA Ops:
  10.2 11.9 %copy-start.2 = (s32[2]{0:T(128)S(1)}, s32[2]{0:T(128)}, u32[]{:S(2)}) copy-start(s32[2]{0:T(128)} %pair_ref.3) | copy-start | bytes 28
  10.2 13.8 %copy-start = (f32[1024,768]{1,0:T(8,128)S(1)}, f32[1024,768]{1,0:T(8,128)}, u32[]{:S(2)}) copy-start(f32[1024,768]{1,0:T(8,128)} %param.38) | copy-start | bytes 9437188
  10.2 125.2 %all-to-all-start = ((bf16[128,48,768]{2,1,0:T(8,128)(2,1)}), bf16[128,48,768]{2,1,0:T(8,128)(2,1)}, u32[]{:S(2)}, u32[]{:S(2)}) async-start(bf16[128,48,768]{2,1,0:T(8,128)(2,1)} %bitcast.6), calls=%async_computation | async-start | bytes 18874368 | tf_op jit(solution)/shard_map/all_to_all | solution.py:288
  146.6 3.6 %collective-permute-start.4 = (f32[2,1,2048]{2,1,0:T(1,128)S(1)}, f32[2,1,2048]{2,1,0:T(1,128)}, u32[]{:S(2)}, u32[]{:S(2)}) collective-permute-start(f32[2,1,2048]{2,1,0:T(1,128)S(1)} %param.5), channel_id=1, source_target_pairs={{0,5},{1,4},{2,7},{3,6},{4,1},{5,0},{6,3},{7,2},{8,13},{9,12},{10,... | collective-permute-start | bytes 49160 | tf_op jit(solution)/shard_map/cond/branch_5_fun/ppermute | solution.py:275
  174.0 29.4 %all-to-all-start.1 = ((f32[128,1,256]{2,1,0:T(1,128)}), f32[128,1,256]{2,1,0:T(1,128)S(1)}, u32[]{:S(2)}, u32[]{:S(2)}) async-start(f32[128,1,256]{2,1,0:T(1,128)} %get-tuple-element.85), calls=%async_computation.1 | async-start | bytes 262144 | tf_op jit(solution)/shard_map/all_to_all | solution.py:299
  186.3 4.6 %collective-permute-start.16 = (f32[2,1,2048]{2,1,0:T(1,128)S(1)}, f32[2,1,2048]{2,1,0:T(1,128)}, u32[]{:S(2)}, u32[]{:S(2)}) collective-permute-start(f32[2,1,2048]{2,1,0:T(1,128)S(1)} %param.18), channel_id=1, source_target_pairs={{0,2},{1,3},{2,0},{3,1},{4,6},{5,7},{6,4},{7,5},{8,10},{9,11},{10,... | collective-permute-start | bytes 49160 | tf_op jit(solution)/shard_map/cond/branch_2_fun/ppermute | solution.py:275
  203.5 0.7 copy-start.1

commit v3 on v2

--- a/solution.py
+++ b/solution.py
@@ -38,7 +38,18 @@
 
 
 def pack_kernel(
-    capacity, pair_ref, ids_ref, rows_ref, out_ref, marks_ref, place_ref, unit_ref, spot_ref, y_ref
+    capacity,
+    pair_ref,
+    ids_ref,
+    rows_ref,
+    tiles_ref,
+    out_ref,
+    marks_ref,
+    place_ref,
+    units_ref,
+    unit_ref,
+    spot_ref,
+    y_ref,
 ):
     g = pl.program_id(0)
     rows = rows_ref.shape[0]
@@ -65,6 +76,7 @@
             spot_ref[:, lanes] = (owner * capacity + place).astype(jnp.int32)
             passed = passed + jnp.sum(piece, axis=1, keepdims=True)
 
+    units_ref[...] = unit_vectors(tiles_ref[...])
     chosen = jnp.where(iota((slots, rows), 0) + g * slots == spot_ref[...], 1.0, 0.0)
     found = jnp.sum(chosen, axis=1, keepdims=True)
     y = dot(chosen.astype(BF16), unit_ref[...], ((1,), (0,)))
@@ -80,8 +92,9 @@
                 out_ref[h, k, 1 + p] = y_ref[pl.ds(pl.multiple_of(start, capacity), capacity), :]
 
 
-def pack(rows, block_ids, pairing, groups, members, capacity, steps):
+def pack(rows, block_ids, centroids, pairing, groups, members, capacity, steps):
     count, width = rows.shape
+    tile_spec = pl.BlockSpec((centroids.shape[0] // steps, width), lambda g: (g, 0))
     devices = groups * members
     return pl.pallas_call(
         functools.partial(pack_kernel, capacity),
@@ -90,6 +103,7 @@
             pl.BlockSpec(memory_space=pltpu.SMEM),
             pl.BlockSpec((1, count), lambda g: (0, 0)),
             pl.BlockSpec((count, width), lambda g: (0, 0)),
+            tile_spec,
         ],
         out_specs=[
             pl.BlockSpec(
@@ -98,11 +112,13 @@
             ),
             pl.BlockSpec((devices, count), lambda g: (0, 0)),
             pl.BlockSpec((1, count), lambda g: (0, 0)),
+            tile_spec,
         ],
         out_shape=[
             jax.ShapeDtypeStruct((groups, members, 1 + PASSES, capacity, width), BF16),
             jax.ShapeDtypeStruct((devices, count), BF16),
             jax.ShapeDtypeStruct((1, count), jnp.int32),
+            jax.ShapeDtypeStruct(centroids.shape, BF16),
         ],
         scratch_shapes=[
             VMEM((count, width), BF16),
@@ -113,7 +129,7 @@
             flops=4 * count * count * width, bytes_accessed=20 << 20, transcendentals=0
         ),
         name="pack",
-    )(pairing, block_ids.reshape(1, count), rows)
+    )(pairing, block_ids.reshape(1, count), rows, centroids)
 
 
 def affinity_kernel(last, inner, tiles_ref, x_ref, aff_ref, total_ref, flag_ref, *rest):
@@ -239,6 +255,14 @@
     )(tiles, aff, got, total, swapped, flag)
 
 
+def thirds(values):
+    high = values.astype(BF16)
+    rest = values - high.astype(F32)
+    middle = rest.astype(BF16)
+    low = (rest - middle.astype(F32)).astype(BF16)
+    return jnp.concatenate([high, middle, low], axis=0)
+
+
 def energy_kernel(capacity, columns, pair_ref, back_ref, marks_ref, place_ref, out_ref):
     devices = back_ref.shape[0]
     across = jnp.where(
@@ -247,13 +271,14 @@
         1.0,
         0.0,
     )
-    total = back_ref[:, 0, :128] + dot(
-        across, back_ref[:, 0, 128:], ((1,), (0,)), lax.Precision.HIGHEST
-    )
-    found = dot(
-        total.T[:capacity], marks_ref[...].astype(F32), ((1,), (0,)), lax.Precision.HIGHEST
-    )
-    mine = jnp.where(iota(found.shape, 0) == place_ref[...], found, 0.0)
+    own = thirds(back_ref[:, 0, :128].T[:capacity])
+    other = thirds(back_ref[:, 0, 128:].T[:capacity])
+    other = dot(other, across.astype(BF16), ((1,), (0,))).astype(BF16)
+    found = dot(jnp.concatenate([own, other], axis=0), marks_ref[...], ((1,), (0,)))
+    sums = found[:capacity]
+    for n in range(1, 6):
+        sums = sums + found[n * capacity : (n + 1) * capacity]
+    mine = jnp.where(iota(sums.shape, 0) == place_ref[...], sums, 0.0)
     out_ref[...] = jnp.log(jnp.sum(mine, axis=0, keepdims=True) / columns)
 
 
@@ -284,7 +309,9 @@
     rows_dev, width = rows.shape
     tile_rows = centroids.shape[0]
     capacity = 2 * rows_dev // devices
-    sent, marks, place = pack(rows, block_ids, pairing, groups, members, capacity, 2)
+    sent, marks, place, tiles = pack(
+        rows, block_ids, centroids, pairing, groups, members, capacity, 4
+    )
     got = lax.all_to_all(
         sent.reshape(devices, (1 + PASSES) * capacity, width),
         ("dp", "blk"),
@@ -292,7 +319,7 @@
         concat_axis=0,
         tiled=True,
     ).reshape(devices, 1 + PASSES, capacity, width)
-    tiles = unit_vectors(centroids)
+    got, pairing = lax.optimization_barrier((got, pairing))
     for p in range(PASSES):
         aff, total, flag, *spread = affinity(tiles, got, p, 1024, 512)
         if spread:

time: 206 us -> 202 us (0.981)
  blocking collectives: 0 us -> 121 us
  waiting for transfers between devices: 115 us -> 4.58 us
  starting transfers between devices: 27.1 us -> 11.7 us
    all_to_all x0 -> x1, blocking collectives: none -> 121 us  [on_device(): lax.all_to_all(sent.reshape(devices, (1 + PASSES) * capacity, width), ('d...]
    all_to_all x1 -> x0, waiting for transfers between devices: 110 us -> none  [on_device(): lax.all_to_all(sent.reshape(devices, (1 + PASSES) * capacity, width), ('d...]
    all_to_all x1 -> x0, starting transfers between devices: 11.9 us -> none  [on_device(): lax.all_to_all(sent.reshape(devices, (1 + PASSES) * capacity, width), ('d...]
    all_to_all x1, starting transfers between devices: 12.3 us -> 6.25 us  [on_device(): lax.all_to_all(spread[0], ('dp', 'blk'), split_axis=0, concat_axis=0, til...]
    ppermute x2, starting transfers between devices: 2.99 us -> 5.46 us  [branch(): lax.ppermute(current, 'blk', [(i, i ^ apart) for i in range(width)])]
  transfers between devices with their start and end apart: 4 -> 3, of which waited for: 3 -> 2; matrix products, arithmetic and copies ran while one was open for 1% -> 0% of each run, Pallas kernels for 6% -> 6%
where the time goes in v3:
time: 202 us; the launch traced here: 200 us
  blocking collectives  121 us (60%)
  Pallas kernels  59.8 us (30%)
  starting transfers between devices  11.7 us (6%)
  waiting for transfers between devices  4.58 us (2%)
    all_to_all x1, blocking collectives, on_device(): lax.all_to_all(sent.reshape(devices, (1 + PASSES) * capacity, width), ('d...  121 us
    pallas_call x2, Pallas kernels, sums(): pl.pallas_call(functools.partial(sums_kernel, last), grid=(2, slots // bl...  25 us
    pallas_call x2, Pallas kernels, affinity(): pl.pallas_call(functools.partial(affinity_kernel, last, inner), grid=(2,...  22.6 us
    pallas_call x1, Pallas kernels, pack(): pl.pallas_call(functools.partial(pack_kernel, capacity), grid=(steps,), i...  10.2 us
    all_to_all x1, starting transfers between devices, on_device(): lax.all_to_all(spread[0], ('dp', 'blk'), split_axis=0, concat_axis=0, til...  6.25 us
    ppermute x2, starting transfers between devices, branch(): lax.ppermute(current, 'blk', [(i, i ^ apart) for i in range(width)])  5.46 us
    ppermute x2, waiting for transfers between devices, branch(): lax.ppermute(current, 'blk', [(i, i ^ apart) for i in range(width)])  4.58 us
  transfers between devices with their start and end apart: 3, of which 2 were waited for; matrix products, arithmetic and copies ran while one was open for 0% of the time, Pallas kernels for 6%

profile of v3, /device:TPU:1, one launch (start us, length us, event | category | flops | bytes accessed | tf_op | source)
XLA Modules:
  0.0 200.5 jit_solution(1816234646792412228)
XLA Ops:
  0.6 10.2 %pack.1 = (bf16[8,16,3,16,768]{4,3,2,1,0:T(8,128)(2,1)}, bf16[128,1024]{1,0:T(8,128)(2,1)}, s32[1,1024]{1,0:T(1,128)}, bf16[1024,768]{1,0:T(8,128)(2,1)}) custom-call(s32[2]{0:T(128)} %pair_ref.2, s32[1,1024]{1,0:T(1,128)} %bitcast.12, bf16[1024,768]{1,0:T(8,128)(2,1)} %rows_ref.1, f32[1024,768]{1,0:T(8,128)} %tiles_ref.1), custom_call_target="tpu_custom_call" | custom-call | flops 3221225472 | bytes 20971520 | tf_op jit(solution)/shard_map/pack/pallas_call | solution.py:99
  10.9 0.0 copy-start.1
  10.9 121.1 %all_to_all.10 = bf16[128,48,768]{2,1,0:T(8,128)(2,1)} all-to-all(bf16[128,48,768]{2,1,0:T(8,128)(2,1)} %bitcast.10), channel_id=1, replica_groups=mesh['dp'=8,'blk'=16] {'dp','blk'}, dimensions={0} | all-to-all | bytes 18874368 | tf_op jit(solution)/shard_map/all_to_all | solution.py:315
  131.9 0.0 copy-done.1
  131.9 0.6 fusion
  133.9 11.3 %affinity.2 = (bf16[2,1024,2048]{2,1,0:T(8,128)(2,1)}, f32[2,1,2048]{2,1,0:T(1,128)S(1)}, f32[2,1,2048]{2,1,0:T(1,128)}) custom-call(bf16[1024,768]{1,0:T(8,128)(2,1)} %get-tuple-element.81.tiles_ref, bf16[128,3,16,768]{3,2,1,0:T(8,128)(2,1)} %bitcast.6), custom_call_target="tpu_custom_call" | custom-call | flops 6442450944 | bytes 16777216 | tf_op jit(solution)/shard_map/affinity/pallas_call | solution.py:178
  145.1 4.2 %conditional.2 = (f32[2,1,2048]{2,1,0:T(1,128)}) conditional(s32[]{:T(128)} %bitcast.3, f32[2,1,2048]{2,1,0:T(1,128)S(1)} %get-tuple-element.85.total_ref, f32[2,1,2048]{2,1,0:T(1,128)S(1)} %get-tuple-element.85.total_ref, f32[2,1,2048]{2,1,0:T(1,128)S(1)} %get-tuple-element.85.total_ref, ...), branch_computations={%region_0.0_spmd, %region_1.0_spmd, %region_2.0_spmd, %region_3.0_... | conditional | bytes 65584 | solution.py:302
  145.1 1.1 collective-permute-start.1
  146.3 3.1 %collective-permute-done.1 = f32[2,1,2048]{2,1,0:T(1,128)} collective-permute-done((f32[2,1,2048]{2,1,0:T(1,128)S(1)}, f32[2,1,2048]{2,1,0:T(1,128)}, u32[]{:S(2)}, u32[]{:S(2)}) %collective-permute-start.1) | collective-permute-done | bytes 16416 | tf_op jit(solution)/shard_map/cond/branch_2_fun/ppermute | solution.py:300
  149.3 12.4 %sums.2.tiles_ref = bf16[1024,768]{1,0:T(8,128)(2,1)} custom-call(bf16[1024,768]{1,0:T(8,128)(2,1)} %get-tuple-element.81.tiles_ref, bf16[2,1024,2048]{2,1,0:T(8,128)(2,1)} %get-tuple-element.84.aff_ref, bf16[128,3,16,768]{3,2,1,0:T(8,128)(2,1)} %bitcast.7, f32[2,1,2048]{2,1,0:T(1,128)S(1)} %get-tuple-element.85.total_ref, ...), custom_call_target="tpu_custom_call" | custom-call | flops 6442450944 | bytes 16777216 | tf_op jit(solution)/shard_map/sums/pallas_call | solution.py:235
  161.8 11.4 %affinity.3 = (bf16[2,1024,2048]{2,1,0:T(8,128)(2,1)}, f32[2,1,2048]{2,1,0:T(1,128)S(1)}, f32[2,1,2048]{2,1,0:T(1,128)}, f32[128,1,256]{2,1,0:T(1,128)}) custom-call(bf16[1024,768]{1,0:T(8,128)(2,1)} %sums.2.tiles_ref, bf16[128,3,16,768]{3,2,1,0:T(8,128)(2,1)} %bitcast.8), custom_call_target="tpu_custom_call" | custom-call | flops 6442450944 | bytes 16777216 | tf_op jit(solution)/shard_map/affinity/pallas_call | solution.py:178
  173.1 6.2 %all-to-all-start.1 = ((f32[128,1,256]{2,1,0:T(1,128)}), f32[128,1,256]{2,1,0:T(1,128)S(1)}, u32[]{:S(2)}, u32[]{:S(2)}) async-start(f32[128,1,256]{2,1,0:T(1,128)} %get-tuple-element.91), calls=%async_computation.1 | async-start | bytes 262144 | tf_op jit(solution)/shard_map/all_to_all | solution.py:326
  179.4 5.9 %conditional.3 = (f32[2,1,2048]{2,1,0:T(1,128)}) conditional(s32[]{:T(128)} %bitcast.4, f32[2,1,2048]{2,1,0:T(1,128)S(1)} %get-tuple-element.89.total_ref, f32[2,1,2048]{2,1,0:T(1,128)S(1)} %get-tuple-element.89.total_ref, f32[2,1,2048]{2,1,0:T(1,128)S(1)} %get-tuple-element.89.total_ref, ...), branch_computations={%region_16.0_spmd, %region_17.0_spmd, %region_18.0_spmd, %region_1... | conditional | bytes 65584 | solution.py:302
  179.4 4.3 %collective-permute-start.27 = (f32[2,1,2048]{2,1,0:T(1,128)S(1)}, f32[2,1,2048]{2,1,0:T(1,128)}, u32[]{:S(2)}, u32[]{:S(2)}) collective-permute-start(f32[2,1,2048]{2,1,0:T(1,128)S(1)} %param.29), channel_id=1, source_target_pairs={{0,13},{1,12},{2,15},{3,14},{4,9},{5,8},{6,11},{7,10},{8,5},{9,4},... | collective-permute-start | bytes 49160 | tf_op jit(solution)/shard_map/cond/branch_13_fun/ppermute | solution.py:300
  183.8 1.5 collective-permute-done.27
  185.3 12.6 %sums.3 = f32[1024,768]{1,0:T(8,128)} custom-call(bf16[1024,768]{1,0:T(8,128)(2,1)} %sums.2.tiles_ref, bf16[2,1024,2048]{2,1,0:T(8,128)(2,1)} %get-tuple-element.88.aff_ref, bf16[128,3,16,768]{3,2,1,0:T(8,128)(2,1)} %bitcast.9, f32[2,1,2048]{2,1,0:T(1,128)S(1)} %get-tuple-element.89.total_ref, f32[2,1,2048]{2,1,0:T(1,128)} %get-tuple-element.97.swapped_ref, ...), custom_call_target="tpu_custom_call" | custom-call | flops 6442450944 | bytes 16777216 | tf_op jit(solution)/shard_map/sums/pallas_call | solution.py:235
  197.8 0.0 all-to-all-done.1.back_ref
  197.8 0.0 copy-start
  197.8 0.6 copy-done
  198.5 2.0 energies.1
Async XLA Ops:
  10.9 121.1 %copy-start.1 = (s32[2]{0:T(128)S(1)}, s32[2]{0:T(128)}, u32[]{:S(2)}) copy-start(s32[2]{0:T(128)} %pair_ref.2) | copy-start | bytes 28
  145.1 4.2 %collective-permute-start.1 = (f32[2,1,2048]{2,1,0:T(1,128)S(1)}, f32[2,1,2048]{2,1,0:T(1,128)}, u32[]{:S(2)}, u32[]{:S(2)}) collective-permute-start(f32[2,1,2048]{2,1,0:T(1,128)S(1)} %param.2), channel_id=1, source_target_pairs={{0,2},{1,3},{2,0},{3,1},{4,6},{5,7},{6,4},{7,5},{8,10},{9,11},{10,... | collective-permute-start | bytes 49160 | tf_op jit(solution)/shard_map/cond/branch_2_fun/ppermute | solution.py:300
  173.1 24.7 %all-to-all-start.1 = ((f32[128,1,256]{2,1,0:T(1,128)}), f32[128,1,256]{2,1,0:T(1,128)S(1)}, u32[]{:S(2)}, u32[]{:S(2)}) async-start(f32[128,1,256]{2,1,0:T(1,128)} %get-tuple-element.91), calls=%async_computation.1 | async-start | bytes 262144 | tf_op jit(solution)/shard_map/all_to_all | solution.py:326
  179.4 5.8 %collective-permute-start.27 = (f32[2,1,2048]{2,1,0:T(1,128)S(1)}, f32[2,1,2048]{2,1,0:T(1,128)}, u32[]{:S(2)}, u32[]{:S(2)}) collective-permute-start(f32[2,1,2048]{2,1,0:T(1,128)S(1)} %param.29), channel_id=1, source_target_pairs={{0,13},{1,12},{2,15},{3,14},{4,9},{5,8},{6,11},{7,10},{8,5},{9,4},... | collective-permute-start | bytes 49160 | tf_op jit(solution)/shard_map/cond/branch_13_fun/ppermute | solution.py:300
  197.8 0.6 copy-start

commit v4 on v3

--- a/solution.py
+++ b/solution.py
@@ -44,6 +44,7 @@
     rows_ref,
     tiles_ref,
     out_ref,
+    late_ref,
     marks_ref,
     place_ref,
     units_ref,
@@ -89,7 +90,11 @@
             out_ref[h, k, 0] = y_ref[base + k * capacity : base + (k + 1) * capacity, :]
             for p in range(PASSES):
                 start = base + jnp.bitwise_xor(pair_ref[p], k) * capacity
-                out_ref[h, k, 1 + p] = y_ref[pl.ds(pl.multiple_of(start, capacity), capacity), :]
+                chunk = y_ref[pl.ds(pl.multiple_of(start, capacity), capacity), :]
+                if p == 0:
+                    out_ref[h, k, 1] = chunk
+                else:
+                    late_ref[h, k] = chunk
 
 
 def pack(rows, block_ids, centroids, pairing, groups, members, capacity, steps):
@@ -107,15 +112,16 @@
         ],
         out_specs=[
             pl.BlockSpec(
-                (groups // steps, members, 1 + PASSES, capacity, width),
-                lambda g: (g, 0, 0, 0, 0),
+                (groups // steps, members, 2, capacity, width), lambda g: (g, 0, 0, 0, 0)
             ),
+            pl.BlockSpec((groups // steps, members, capacity, width), lambda g: (g, 0, 0, 0)),
             pl.BlockSpec((devices, count), lambda g: (0, 0)),
             pl.BlockSpec((1, count), lambda g: (0, 0)),
             tile_spec,
         ],
         out_shape=[
-            jax.ShapeDtypeStruct((groups, members, 1 + PASSES, capacity, width), BF16),
+            jax.ShapeDtypeStruct((groups, members, 2, capacity, width), BF16),
+            jax.ShapeDtypeStruct((groups, members, capacity, width), BF16),
             jax.ShapeDtypeStruct((devices, count), BF16),
             jax.ShapeDtypeStruct((1, count), jnp.int32),
             jax.ShapeDtypeStruct(centroids.shape, BF16),
@@ -132,82 +138,127 @@
     )(pairing, block_ids.reshape(1, count), rows, centroids)
 
 
-def affinity_kernel(last, inner, tiles_ref, x_ref, aff_ref, total_ref, flag_ref, *rest):
-    wide_ref = rest[-1]
+def fill_wide(wide_ref, tiles_ref):
     tile_rows, width = tiles_ref.shape
-    capacity = x_ref.shape[2]
-    block = aff_ref.shape[2]
-
+    wide_ref[:tile_rows] = tiles_ref[...]
+    wide_ref[tile_rows:] = jnp.where(iota((FLAG_ROWS, width), 1) == 0, 1.0, 0.0).astype(BF16)
+
+
+def score(inner, wide_ref, x_ref, aff_ref, start=0):
+    tile_rows, block = aff_ref.shape[1:]
+    width = wide_ref.shape[1]
+    count = inner // x_ref.shape[2]
+    for n in range(block // inner):
+        lanes = slice(n * inner, (n + 1) * inner)
+        x = x_ref[pl.ds(start + n * count, count)].reshape(inner, width)
+        scores = dot(wide_ref[...], x, ((1,), (1,)))
+        aff = jnp.exp2((KAPPA * math.log2(math.e)) * scores[:tile_rows])
+        aff_ref[0, :, lanes] = aff.astype(BF16)
+        yield lanes, jnp.sum(aff, axis=0, keepdims=True), scores[tile_rows:][:1]
+
+
+def spread(total, lanes, capacity, out_ref):
+    for v in range(total.shape[1] // 128):
+        piece = total[:, v * 128 : (v + 1) * 128]
+        for k in range(128 // capacity):
+            source = (lanes.start + v * 128) // capacity + k
+            out_ref[source, :, -128:] = pltpu.roll(piece, (128 - k * capacity) % 128, 1)
+
+
+def first_kernel(inner, tiles_ref, x_ref, aff_ref, total_ref, flag_ref, wide_ref):
     @pl.when((pl.program_id(0) == 0) & (pl.program_id(1) == 0))
     def _():
-        wide_ref[:tile_rows] = tiles_ref[...]
-        wide_ref[tile_rows:] = jnp.where(
-            iota((FLAG_ROWS, width), 1) == 0, 1.0, 0.0
-        ).astype(BF16)
-
-    count = inner // capacity
-    for n in range(block // inner):
-        lanes = slice(n * inner, (n + 1) * inner)
-        x = x_ref[n * count : (n + 1) * count].reshape(inner, width)
-        scores = dot(wide_ref[...], x, ((1,), (1,)))
-        aff = jnp.exp2((KAPPA * math.log2(math.e)) * scores[:tile_rows])
-        total = jnp.sum(aff, axis=0, keepdims=True)
+        fill_wide(wide_ref, tiles_ref)
+
+    for lanes, total, flag in score(inner, wide_ref, x_ref, aff_ref):
         total_ref[0, :, lanes] = total
-        flag_ref[0, :, lanes] = scores[tile_rows : tile_rows + 1]
-        aff_ref[0, :, lanes] = aff.astype(BF16)
-        if last:
-            for v in range(inner // 128):
-                piece = total[:, v * 128 : (v + 1) * 128]
-                for k in range(128 // capacity):
-                    source = (n * inner + v * 128) // capacity + k
-                    rest[0][source] = pltpu.roll(piece, (128 - k * capacity) % 128, 1)
-
-
-def affinity(tiles, got, p, block, inner):
+        flag_ref[0, :, lanes] = flag
+
+
+def own_kernel(inner, tiles_ref, x_ref, aff_ref, total_ref, spread_ref, wide_ref):
+    for lanes, total, _ in score(inner, tiles_ref, x_ref, aff_ref):
+        total_ref[0, :, lanes] = total
+        spread(total, lanes, x_ref.shape[2], spread_ref)
+
+
+def other_kernel(
+    inner,
+    tiles_ref,
+    x_ref,
+    own_total_ref,
+    own_flag_ref,
+    own_spread_ref,
+    _,
+    aff_ref,
+    total_ref,
+    flag_ref,
+    spread_ref,
+    wide_ref,
+):
+    @pl.when(pl.program_id(1) == 0)
+    def _():
+        fill_wide(wide_ref, tiles_ref)
+
+    total_ref[0] = own_total_ref[0]
+    flag_ref[0] = own_flag_ref[0]
+    spread_ref[:, :, :128] = own_spread_ref[...]
+    start = pl.program_id(1) * (aff_ref.shape[2] // x_ref.shape[2])
+    for lanes, total, flag in score(inner, wide_ref, x_ref, aff_ref, start):
+        total_ref[1, :, lanes] = total
+        flag_ref[1, :, lanes] = flag
+        spread(total, lanes, x_ref.shape[2], spread_ref)
+
+
+def affinity(kernel, tiles, x, kinds, extra, block, inner):
     tile_rows, width = tiles.shape
-    sources, _, capacity, _ = got.shape
+    sources, _, capacity, _ = x.shape
     slots = sources * capacity
-    last = p == PASSES - 1
+    count = block // capacity
+    row_shape = jax.ShapeDtypeStruct((kinds, 1, slots), F32)
     row_spec = pl.BlockSpec((1, 1, block), lambda c, i: (c, 0, i))
-    row_shape = jax.ShapeDtypeStruct((2, 1, slots), F32)
-    out_specs = [pl.BlockSpec((1, tile_rows, block), lambda c, i: (c, 0, i)), row_spec, row_spec]
-    out_shape = [jax.ShapeDtypeStruct((2, tile_rows, slots), BF16), row_shape, row_shape]
-    if last:
-        out_specs.append(pl.BlockSpec((block // capacity, 1, 128), lambda c, i: (i, 0, c)))
-        out_shape.append(jax.ShapeDtypeStruct((sources, 1, 256), F32))
+    both_shape = jax.ShapeDtypeStruct((2, 1, slots), F32)
+    both_spec = pl.BlockSpec((2, 1, block), lambda c, i: (0, 0, i))
+    spread_spec = pl.BlockSpec((count, 1, 128), lambda c, i: (i, 0, 0))
+    at = 1 if kernel is other_kernel else 0
+    out_specs = [pl.BlockSpec((1, tile_rows, block), lambda c, i: (c + at, 0, i))]
+    out_shape = [jax.ShapeDtypeStruct((2, tile_rows, slots), BF16)]
+    extra_specs = []
+    x_spec = pl.BlockSpec((count, 1, capacity, width), lambda c, i: (i, c, 0, 0))
+    if kernel is first_kernel:
+        out_specs += [row_spec, row_spec]
+        out_shape += [row_shape, row_shape]
+    elif kernel is own_kernel:
+        out_specs += [row_spec, spread_spec]
+        out_shape += [row_shape, jax.ShapeDtypeStruct((sources, 1, 128), F32)]
+    else:
+        x_spec = pl.BlockSpec(memory_space=VMEM)
+        extra_specs = [row_spec, row_spec, spread_spec, pl.BlockSpec(memory_space=pl.ANY)]
+        out_specs += [both_spec, both_spec, pl.BlockSpec((count, 1, 256), lambda c, i: (i, 0, 0))]
+        out_shape += [both_shape, both_shape, jax.ShapeDtypeStruct((sources, 1, 256), F32)]
     return pl.pallas_call(
-        functools.partial(affinity_kernel, last, inner),
-        grid=(2, slots // block),
+        functools.partial(kernel, inner),
+        grid=(kinds, slots // block),
         in_specs=[
             pl.BlockSpec((tile_rows, width), lambda c, i: (0, 0)),
-            pl.BlockSpec(
-                (block // capacity, 1, capacity, width), lambda c, i: (i, c * (1 + p), 0, 0)
-            ),
-        ],
+            x_spec,
+        ]
+        + extra_specs,
         out_specs=out_specs,
         out_shape=out_shape,
+        input_output_aliases={5: 0} if at else {},
         scratch_shapes=[VMEM((tile_rows + FLAG_ROWS, width), BF16)],
         cost_estimate=pl.CostEstimate(
-            flops=4 * slots * tile_rows * width,
-            bytes_accessed=16 << 20,
-            transcendentals=2 * slots * tile_rows,
+            flops=2 * kinds * slots * tile_rows * width,
+            bytes_accessed=kinds * (8 << 20),
+            transcendentals=kinds * slots * tile_rows,
         ),
         name="affinity",
-    )(tiles, got)
-
-
-def sums_kernel(
-    last, tiles_ref, aff_ref, x_ref, total_ref, swapped_ref, flag_ref, out_ref, acc_ref, count_ref
-):
-    c, i = pl.program_id(0), pl.program_id(1)
-    tile_rows, width = tiles_ref.shape
+    )(tiles, x, *extra)
+
+
+def add_block(aff_ref, x, total_ref, swapped_ref, flag_ref, acc_ref, count_ref):
     block = aff_ref.shape[2]
-
-    @pl.when((c == 0) & (i == 0))
-    def _():
-        acc_ref[...] = jnp.zeros_like(acc_ref)
-        count_ref[...] = jnp.zeros_like(count_ref)
-
+    width = acc_ref.shape[1]
     total = total_ref[0] + swapped_ref[0]
     inverse = jnp.where(flag_ref[0] < LIMIT, 1.0 / total, 0.0)
     weights = aff_ref[0].astype(F32) * inverse
@@ -215,7 +266,26 @@
     for n in range(1, block // 128):
         part = part + weights[:, n * 128 : (n + 1) * 128]
     count_ref[...] += part
-    acc_ref[...] += dot(weights.astype(BF16), x_ref[...].reshape(-1, width), ((1,), (0,)))
+    acc_ref[...] += dot(weights.astype(BF16), x.reshape(-1, width), ((1,), (0,)))
+
+
+def sums_kernel(last, tiles_ref, total_ref, swapped_ref, flag_ref, aff_ref, *rest):
+    *xs, out_ref, acc_ref, count_ref = rest
+    c, i = pl.program_id(0), pl.program_id(1)
+    width = tiles_ref.shape[1]
+
+    @pl.when((c == 0) & (i == 0))
+    def _():
+        acc_ref[...] = jnp.zeros_like(acc_ref)
+        count_ref[...] = jnp.zeros_like(count_ref)
+
+    for kind, x_ref in enumerate(xs):
+
+        @pl.when((c == kind) | (len(xs) == 1))
+        def _():
+            per = aff_ref.shape[2] // x_ref.shape[2]
+            x = x_ref[pl.ds(i * per, per)] if kind else x_ref[...]
+            add_block(aff_ref, x, total_ref, swapped_ref, flag_ref, acc_ref, count_ref)
 
     @pl.when((c == pl.num_programs(0) - 1) & (i == pl.num_programs(1) - 1))
     def _():
@@ -226,25 +296,31 @@
         out_ref[...] = centers if last else unit_vectors(centers)
 
 
-def sums(tiles, aff, got, total, swapped, flag, p, block):
+def sums(tiles, total, swapped, flag, aff, xs, last, block):
     tile_rows, width = tiles.shape
-    sources, _, capacity, _ = got.shape
+    sources, _, capacity, _ = xs[0].shape
     slots = sources * capacity
-    last = p == PASSES - 1
+    steps = slots // block
     row_spec = pl.BlockSpec((1, 1, block), lambda c, i: (c, 0, i))
+    x_shape = (block // capacity, 1, capacity, width)
+    if len(xs) == 1:
+        x_specs = [pl.BlockSpec(x_shape, lambda c, i: (i, c, 0, 0))]
+    else:
+        x_specs = [
+            pl.BlockSpec(x_shape, lambda c, i: (jnp.where(c == 0, i, steps - 1), 0, 0, 0)),
+            pl.BlockSpec(memory_space=VMEM),
+        ]
     return pl.pallas_call(
         functools.partial(sums_kernel, last),
-        grid=(2, slots // block),
+        grid=(2, steps),
         in_specs=[
             pl.BlockSpec((tile_rows, width), lambda c, i: (0, 0)),
-            pl.BlockSpec((1, tile_rows, block), lambda c, i: (c, 0, i)),
-            pl.BlockSpec(
-                (block // capacity, 1, capacity, width), lambda c, i: (i, c * (1 + p), 0, 0)
-            ),
             row_spec,
             pl.BlockSpec((1, 1, block), lambda c, i: (1 - c, 0, i)),
             row_spec,
-        ],
+            pl.BlockSpec((1, tile_rows, block), lambda c, i: (c, 0, i)),
+        ]
+        + x_specs,
         out_specs=pl.BlockSpec((tile_rows, width), lambda c, i: (0, 0)),
         out_shape=jax.ShapeDtypeStruct((tile_rows, width), F32 if last else BF16),
         scratch_shapes=[VMEM((tile_rows, width), F32), VMEM((tile_rows, 128), F32)],
@@ -252,7 +328,7 @@
             flops=4 * slots * tile_rows * width, bytes_accessed=16 << 20, transcendentals=0
         ),
         name="sums",
-    )(tiles, aff, got, total, swapped, flag)
+    )(tiles, total, swapped, flag, aff, *xs)
 
 
 def thirds(values):
@@ -309,27 +385,38 @@
     rows_dev, width = rows.shape
     tile_rows = centroids.shape[0]
     capacity = 2 * rows_dev // devices
-    sent, marks, place, tiles = pack(
+    sent, late, marks, place, tiles = pack(
         rows, block_ids, centroids, pairing, groups, members, capacity, 4
     )
-    got = lax.all_to_all(
-        sent.reshape(devices, (1 + PASSES) * capacity, width),
-        ("dp", "blk"),
-        split_axis=0,
-        concat_axis=0,
-        tiled=True,
-    ).reshape(devices, 1 + PASSES, capacity, width)
+
+    def exchanged(value, slots):
+        got = lax.all_to_all(
+            value.reshape(devices, -1, value.shape[-1]),
+            ("dp", "blk"),
+            split_axis=0,
+            concat_axis=0,
+            tiled=True,
+        )
+        return got.reshape(devices, slots, -1, value.shape[-1])
+
+    got = exchanged(sent, 2)
     got, pairing = lax.optimization_barrier((got, pairing))
-    for p in range(PASSES):
-        aff, total, flag, *spread = affinity(tiles, got, p, 1024, 512)
-        if spread:
-            back = lax.all_to_all(
-                spread[0], ("dp", "blk"), split_axis=0, concat_axis=0, tiled=True
-            )
-        swapped = partner_swap(total, pairing[p], members)
-        tiles = sums(tiles, aff, got, total, swapped, flag, p, 1024)
+    aff, total, flag = affinity(first_kernel, tiles, got, 2, (), 1024, 512)
+    swapped = partner_swap(total, pairing[0], members)
+    swapped, late = lax.optimization_barrier((swapped, late))
+    got_late = pltpu.with_memory_space_constraint(exchanged(late, 1), VMEM)
+    tiles = sums(tiles, total, swapped, flag, aff, (got,), False, 1024)
+    aff, own_total, own_spread = affinity(own_kernel, tiles, got, 1, (), 1024, 512)
+    aff, total, flag, parts = affinity(
+        other_kernel, tiles, got_late, 1, (own_total, flag, own_spread, aff), 1024, 512
+    )
+    swapped = partner_swap(total, pairing[1], members)
+    swapped, parts = lax.optimization_barrier((swapped, parts))
+    back = exchanged(parts, 1).reshape(devices, 1, 256)
+    back = pltpu.with_memory_space_constraint(back, VMEM)
+    centers = sums(tiles, total, swapped, flag, aff, (got, got_late), True, 1024)
     energy = energies(pairing, back, marks, place, capacity, 2.0 * tile_rows)
-    return (tiles, energy.reshape(rows_dev))
+    return (centers, energy.reshape(rows_dev))
 
 
 def solution(mesh):

time: 202 us -> 195 us (0.965)
  blocking collectives: 121 us -> 86.4 us
  waiting for transfers between devices: 4.58 us -> 26.4 us
  starting transfers between devices: 11.7 us -> 16.5 us
  Pallas kernels: 59.8 us -> 62.4 us
    all_to_all x1, blocking collectives: 121 us -> 86.4 us  [exchanged(): lax.all_to_all(value.reshape(devices, -1, value.shape[-1]), ('dp', 'blk')...]
    all_to_all x1 -> x2, waiting for transfers between devices: 0.01 us -> 20.1 us  [exchanged(): lax.all_to_all(value.reshape(devices, -1, value.shape[-1]), ('dp', 'blk')...]
    all_to_all x1 -> x2, starting transfers between devices: 6.25 us -> 12.5 us  [exchanged(): lax.all_to_all(value.reshape(devices, -1, value.shape[-1]), ('dp', 'blk')...]
    pallas_call x4 -> x5, Pallas kernels: 47.6 us -> 50.3 us  [the longest x3 25.3 us: affinity(): pl.pallas_call(functools.partial(kernel, inner), grid=(kinds, slots // bl...]
  transfers between devices with their start and end apart: 3 -> 4, of which waited for: 2 -> 3; matrix products, arithmetic and copies ran while one was open for 0% -> 0% of each run, Pallas kernels for 6% -> 17%
where the time goes in v4:
time: 195 us; the launch traced here: 194 us
  blocking collectives  86.4 us (44%)
  Pallas kernels  62.4 us (32%)
  waiting for transfers between devices  26.4 us (14%)
  starting transfers between devices  16.5 us (8%)
  between operations  2 us (1%)
    all_to_all x1, blocking collectives, exchanged(): lax.all_to_all(value.reshape(devices, -1, value.shape[-1]), ('dp', 'blk')...  86.4 us
    pallas_call x3, Pallas kernels, affinity(): pl.pallas_call(functools.partial(kernel, inner), grid=(kinds, slots // bl...  25.3 us
    pallas_call x2, Pallas kernels, sums(): pl.pallas_call(functools.partial(sums_kernel, last), grid=(2, steps), in_...  25 us
    all_to_all x2, waiting for transfers between devices, exchanged(): lax.all_to_all(value.reshape(devices, -1, value.shape[-1]), ('dp', 'blk')...  20.1 us
    all_to_all x2, starting transfers between devices, exchanged(): lax.all_to_all(value.reshape(devices, -1, value.shape[-1]), ('dp', 'blk')...  12.5 us
    pallas_call x1, Pallas kernels, pack(): pl.pallas_call(functools.partial(pack_kernel, capacity), grid=(steps,), i...  10.2 us
    ppermute x2, waiting for transfers between devices, branch(): lax.ppermute(current, 'blk', [(i, i ^ apart) for i in range(width)])  6.32 us
    ppermute x2, starting transfers between devices, branch(): lax.ppermute(current, 'blk', [(i, i ^ apart) for i in range(width)])  3.97 us
  transfers between devices with their start and end apart: 4, of which 3 were waited for; matrix products, arithmetic and copies ran while one was open for 0% of the time, Pallas kernels for 17%

profile of v4, /device:TPU:1, one launch (start us, length us, event | category | flops | bytes accessed | tf_op | source)
XLA Modules:
  0.0 194.4 jit_solution(17531878742810810)
XLA Ops:
  0.6 10.2 %pack.1 = (bf16[8,16,2,16,768]{4,3,2,1,0:T(8,128)(2,1)}, bf16[8,16,16,768]{3,2,1,0:T(8,128)(2,1)}, bf16[128,1024]{1,0:T(8,128)(2,1)}, s32[1,1024]{1,0:T(1,128)}, bf16[1024,768]{1,0:T(8,128)(2,1)}) custom-call(s32[2]{0:T(128)} %pair_ref.2, s32[1,1024]{1,0:T(1,128)} %bitcast.17, bf16[1024,768]{1,0:T(8,128)(2,1)} %rows_ref.1, f32[1024,768]{1,0:T(8,128)} %tiles_ref.1), custom_call_target="tpu_custom_call" | custom-call | flops 3221225472 | bytes 20971520 | tf_op jit(solution)/shard_map/pack/pallas_call | solution.py:104
  10.8 0.0 copy-start
  10.8 86.4 %all_to_all.15 = bf16[128,32,768]{2,1,0:T(8,128)(2,1)} all-to-all(bf16[128,32,768]{2,1,0:T(8,128)(2,1)} %bitcast.14), channel_id=1, replica_groups=mesh['dp'=8,'blk'=16] {'dp','blk'}, dimensions={0} | all-to-all | bytes 12582912 | tf_op jit(solution)/shard_map/all_to_all | solution.py:393
  97.3 0.0 copy-done
  97.3 0.6 fusion
  97.8 11.3 %affinity.3 = (bf16[2,1024,2048]{2,1,0:T(8,128)(2,1)}, f32[2,1,2048]{2,1,0:T(1,128)S(1)}, f32[2,1,2048]{2,1,0:T(1,128)}) custom-call(bf16[1024,768]{1,0:T(8,128)(2,1)} %get-tuple-element.89.tiles_ref, bf16[128,2,16,768]{3,2,1,0:T(8,128)(2,1)} %bitcast.10), custom_call_target="tpu_custom_call" | custom-call | flops 6442450944 | bytes 16777216 | tf_op jit(solution)/shard_map/affinity/pallas_call | solution.py:238
  109.8 4.0 %conditional.2 = (f32[2,1,2048]{2,1,0:T(1,128)}) conditional(s32[]{:T(128)} %bitcast.3, f32[2,1,2048]{2,1,0:T(1,128)S(1)} %get-tuple-element.92.total_ref, f32[2,1,2048]{2,1,0:T(1,128)S(1)} %get-tuple-element.92.total_ref, f32[2,1,2048]{2,1,0:T(1,128)S(1)} %get-tuple-element.92.total_ref, ...), branch_computations={%region_0.0_spmd, %region_1.0_spmd, %region_2.0_spmd, %region_3.0_... | conditional | bytes 65584 | solution.py:378
  109.9 1.7 collective-permute-start.2
  111.6 2.3 %collective-permute-done.2 = f32[2,1,2048]{2,1,0:T(1,128)} collective-permute-done((f32[2,1,2048]{2,1,0:T(1,128)S(1)}, f32[2,1,2048]{2,1,0:T(1,128)}, u32[]{:S(2)}, u32[]{:S(2)}) %collective-permute-start.2) | collective-permute-done | bytes 16416 | tf_op jit(solution)/shard_map/cond/branch_3_fun/ppermute | solution.py:376
  113.8 6.1 %all-to-all-start.1 = ((bf16[128,16,768]{2,1,0:T(8,128)(2,1)}), bf16[128,16,768]{2,1,0:T(8,128)(2,1)S(1)}, u32[]{:S(2)}, u32[]{:S(2)}) async-start(bf16[128,16,768]{2,1,0:T(8,128)(2,1)} %bitcast.15), calls=%async_computation.1 | async-start | bytes 6291456 | tf_op jit(solution)/shard_map/all_to_all | solution.py:393
  120.6 12.5 %sums.2.tiles_ref = bf16[1024,768]{1,0:T(8,128)(2,1)} custom-call(bf16[1024,768]{1,0:T(8,128)(2,1)} %get-tuple-element.89.tiles_ref, f32[2,1,2048]{2,1,0:T(1,128)S(1)} %get-tuple-element.92.total_ref, f32[2,1,2048]{2,1,0:T(1,128)} %get-tuple-element.112.swapped_ref, f32[2,1,2048]{2,1,0:T(1,128)} %get-tuple-element.96.flag_ref.own_flag_ref, ...), custom_call_target="tpu_custom_call" | custom-call | flops 6442450944 | bytes 16777216 | tf_op jit(solution)/shard_map/sums/pallas_call | solution.py:313
  133.1 7.1 %affinity.4 = (bf16[2,1024,2048]{2,1,0:T(8,128)(2,1)}, f32[1,1,2048]{2,1,0:T(1,128)}, f32[128,1,128]{2,1,0:T(1,128)}) custom-call(bf16[1024,768]{1,0:T(8,128)(2,1)} %sums.2.tiles_ref, bf16[128,2,16,768]{3,2,1,0:T(8,128)(2,1)} %bitcast.12), custom_call_target="tpu_custom_call" | custom-call | flops 3221225472 | bytes 8388608 | tf_op jit(solution)/shard_map/affinity/pallas_call | solution.py:238
  140.2 20.1 %all-to-all-done.1 = bf16[128,16,768]{2,1,0:T(8,128)(2,1)S(1)} async-done(((bf16[128,16,768]{2,1,0:T(8,128)(2,1)}), bf16[128,16,768]{2,1,0:T(8,128)(2,1)S(1)}, u32[]{:S(2)}, u32[]{:S(2)}) %all-to-all-start.1) | async-done | bytes 3145760 | tf_op jit(solution)/shard_map/all_to_all | solution.py:393
  160.3 6.9 %affinity.5 = (bf16[2,1024,2048]{2,1,0:T(8,128)(2,1)}, f32[2,1,2048]{2,1,0:T(1,128)S(1)}, f32[2,1,2048]{2,1,0:T(1,128)}, f32[128,1,256]{2,1,0:T(1,128)}) custom-call(bf16[1024,768]{1,0:T(8,128)(2,1)} %sums.2.tiles_ref, bf16[128,1,16,768]{3,2,1,0:T(8,128)(2,1)S(1)} %bitcast.8, ...), custom_call_target="tpu_custom_call", output_to_operand_aliasing={{0}: (5, {})} | custom-call | flops 3221225472 | bytes 8388608 | tf_op jit(solution)/shard_map/affinity/pallas_call | solution.py:238
  167.2 6.3 %conditional.3 = (f32[2,1,2048]{2,1,0:T(1,128)}) conditional(s32[]{:T(128)} %bitcast.6, f32[2,1,2048]{2,1,0:T(1,128)S(1)} %get-tuple-element.102.total_ref, f32[2,1,2048]{2,1,0:T(1,128)S(1)} %get-tuple-element.102.total_ref, f32[2,1,2048]{2,1,0:T(1,128)S(1)} %get-tuple-element.102.total_ref, ...), branch_computations={%region_16.0_spmd, %region_17.0_spmd, %region_18.0_spmd, %region_1... | conditional | bytes 65584 | solution.py:378
  167.2 2.3 %collective-permute-start.28 = (f32[2,1,2048]{2,1,0:T(1,128)S(1)}, f32[2,1,2048]{2,1,0:T(1,128)}, u32[]{:S(2)}, u32[]{:S(2)}) collective-permute-start(f32[2,1,2048]{2,1,0:T(1,128)S(1)} %param.30), channel_id=1, source_target_pairs={{0,14},{1,15},{2,12},{3,13},{4,10},{5,11},{6,8},{7,9},{8,6},{9,7},... | collective-permute-start | bytes 49160 | tf_op jit(solution)/shard_map/cond/branch_14_fun/ppermute | solution.py:376
  169.5 4.0 %collective-permute-done.28 = f32[2,1,2048]{2,1,0:T(1,128)} collective-permute-done((f32[2,1,2048]{2,1,0:T(1,128)S(1)}, f32[2,1,2048]{2,1,0:T(1,128)}, u32[]{:S(2)}, u32[]{:S(2)}) %collective-permute-start.28) | collective-permute-done | bytes 16416 | tf_op jit(solution)/shard_map/cond/branch_14_fun/ppermute | solution.py:376
  173.5 6.4 %all-to-all-start.2 = ((f32[128,1,256]{2,1,0:T(1,128)}), f32[128,1,256]{2,1,0:T(1,128)S(1)}, u32[]{:S(2)}, u32[]{:S(2)}) async-start(f32[128,1,256]{2,1,0:T(1,128)} %get-tuple-element.107), calls=%async_computation.2 | async-start | bytes 262144 | tf_op jit(solution)/shard_map/all_to_all | solution.py:393
  179.9 12.5 %sums.3 = f32[1024,768]{1,0:T(8,128)} custom-call(bf16[1024,768]{1,0:T(8,128)(2,1)} %sums.2.tiles_ref, f32[2,1,2048]{2,1,0:T(1,128)S(1)} %get-tuple-element.102.total_ref, f32[2,1,2048]{2,1,0:T(1,128)} %get-tuple-element.113.swapped_ref, f32[2,1,2048]{2,1,0:T(1,128)} %get-tuple-element.105.flag_ref, bf16[2,1024,2048]{2,1,0:T(8,128)(2,1)} %get-tuple-element.106.aff_ref, ...), custom_call_target="tpu_custom_call" | custom-call | flops 6442450944 | bytes 16777216 | tf_op jit(solution)/shard_map/sums/pallas_call | solution.py:313
  192.4 0.0 all-to-all-done.2.back_ref
  192.4 2.0 %energies.1 = f32[1,1024]{1,0:T(1,128)} custom-call(s32[2]{0:T(128)} %pair_ref.2, f32[128,1,256]{2,1,0:T(1,128)S(1)} %all-to-all-done.2.back_ref, bf16[128,1024]{1,0:T(8,128)(2,1)} %get-tuple-element.108.marks_ref, s32[1,1024]{1,0:T(1,128)} %get-tuple-element.109.place_ref), custom_call_target="tpu_custom_call" | custom-call | tf_op jit(solution)/shard_map/energies/pallas_call | solution.py:363
Async XLA Ops:
  10.8 86.4 %copy-start = (s32[2]{0:T(128)S(1)}, s32[2]{0:T(128)}, u32[]{:S(2)}) copy-start(s32[2]{0:T(128)} %pair_ref.2) | copy-start | bytes 28
  109.9 4.0 %collective-permute-start.2 = (f32[2,1,2048]{2,1,0:T(1,128)S(1)}, f32[2,1,2048]{2,1,0:T(1,128)}, u32[]{:S(2)}, u32[]{:S(2)}) collective-permute-start(f32[2,1,2048]{2,1,0:T(1,128)S(1)} %param.3), channel_id=1, source_target_pairs={{0,3},{1,2},{2,1},{3,0},{4,7},{5,6},{6,5},{7,4},{8,11},{9,10},{10,... | collective-permute-start | bytes 49160 | tf_op jit(solution)/shard_map/cond/branch_3_fun/ppermute | solution.py:376
  113.8 46.5 %all-to-all-start.1 = ((bf16[128,16,768]{2,1,0:T(8,128)(2,1)}), bf16[128,16,768]{2,1,0:T(8,128)(2,1)S(1)}, u32[]{:S(2)}, u32[]{:S(2)}) async-start(bf16[128,16,768]{2,1,0:T(8,128)(2,1)} %bitcast.15), calls=%async_computation.1 | async-start | bytes 6291456 | tf_op jit(solution)/shard_map/all_to_all | solution.py:393
  167.2 6.3 %collective-permute-start.28 = (f32[2,1,2048]{2,1,0:T(1,128)S(1)}, f32[2,1,2048]{2,1,0:T(1,128)}, u32[]{:S(2)}, u32[]{:S(2)}) collective-permute-start(f32[2,1,2048]{2,1,0:T(1,128)S(1)} %param.30), channel_id=1, source_target_pairs={{0,14},{1,15},{2,12},{3,13},{4,10},{5,11},{6,8},{7,9},{8,6},{9,7},... | collective-permute-start | bytes 49160 | tf_op jit(solution)/shard_map/cond/branch_14_fun/ppermute | solution.py:376
  173.5 18.9 %all-to-all-start.2 = ((f32[128,1,256]{2,1,0:T(1,128)}), f32[128,1,256]{2,1,0:T(1,128)S(1)}, u32[]{:S(2)}, u32[]{:S(2)}) async-start(f32[128,1,256]{2,1,0:T(1,128)} %get-tuple-element.107), calls=%async_computation.2 | async-start | bytes 262144 | tf_op jit(solution)/shard_map/all_to_all | solution.py:393

commit v5 on v4

--- a/solution.py
+++ b/solution.py
@@ -50,6 +50,7 @@
     units_ref,
     unit_ref,
     spot_ref,
+    held_ref,
     y_ref,
 ):
     g = pl.program_id(0)
@@ -76,12 +77,19 @@
             place_ref[:, lanes] = place.astype(jnp.int32)
             spot_ref[:, lanes] = (owner * capacity + place).astype(jnp.int32)
             passed = passed + jnp.sum(piece, axis=1, keepdims=True)
+        held_ref[...] = jnp.broadcast_to(passed, (devices, 128)).astype(BF16)
 
     units_ref[...] = unit_vectors(tiles_ref[...])
-    chosen = jnp.where(iota((slots, rows), 0) + g * slots == spot_ref[...], 1.0, 0.0)
-    found = jnp.sum(chosen, axis=1, keepdims=True)
-    y = dot(chosen.astype(BF16), unit_ref[...], ((1,), (0,)))
-    mark = jnp.where(iota((slots, 128), 1) == 0, ABSENT, 0.0) * (1.0 - found)
+    here = slots // capacity
+    named = marks_ref[pl.ds(pl.multiple_of(g * here, here), here), :]
+    level = jnp.where(iota((capacity, rows), 0) == place_ref[...], 1.0, 0.0).astype(BF16)
+    chosen = jnp.concatenate([level * named[n : n + 1] for n in range(here)], axis=0)
+    whose = (iota((slots, devices), 0) + g * slots) // capacity
+    mine = jnp.where(whose == iota((slots, devices), 1), 1.0, 0.0).astype(BF16)
+    held = dot(mine, held_ref[...], ((1,), (0,)))
+    lacks = (iota((slots, 128), 0) % capacity).astype(F32) >= held
+    y = dot(chosen, unit_ref[...], ((1,), (0,)))
+    mark = jnp.where(lacks & (iota((slots, 128), 1) == 0), ABSENT, 0.0)
     y_ref[...] = y.astype(BF16)
     y_ref[:, :128] = (y[:, :128] + mark).astype(BF16)
     for h in range(groups):
@@ -129,6 +137,7 @@
         scratch_shapes=[
             VMEM((count, width), BF16),
             VMEM((1, count), jnp.int32),
+            VMEM((devices, 128), BF16),
             VMEM((devices * capacity // steps, width), BF16),
         ],
         cost_estimate=pl.CostEstimate(
@@ -270,7 +279,7 @@
 
 
 def sums_kernel(last, tiles_ref, total_ref, swapped_ref, flag_ref, aff_ref, *rest):
-    *xs, out_ref, acc_ref, count_ref = rest
+    *xs, out_ref, acc_ref, count_ref, sems = rest
     c, i = pl.program_id(0), pl.program_id(1)
     width = tiles_ref.shape[1]
 
@@ -289,11 +298,23 @@
 
     @pl.when((c == pl.num_programs(0) - 1) & (i == pl.num_programs(1) - 1))
     def _():
-        counts = jnp.sum(count_ref[...], axis=1, keepdims=True)
-        centers = (
-            math.sqrt(width) * (acc_ref[...] + tiles_ref[...].astype(F32)) / (counts + 1.0)
-        )
-        out_ref[...] = centers if last else unit_vectors(centers)
+        per = tiles_ref.shape[0] // sems.shape[0]
+        copies = []
+        for n in range(sems.shape[0]):
+            part = pl.ds(n * per, per)
+            counts = jnp.sum(count_ref[part], axis=1, keepdims=True)
+            centers = (
+                math.sqrt(width) * (acc_ref[part] + tiles_ref[part].astype(F32)) / (counts + 1.0)
+            )
+            if not last:
+                out_ref[part] = unit_vectors(centers)
+                continue
+            acc_ref[part] = centers
+            copy = pltpu.make_async_copy(acc_ref.at[part], out_ref.at[part], sems.at[n])
+            copy.start()
+            copies.append(copy)
+        for copy in copies:
+            copy.wait()
 
 
 def sums(tiles, total, swapped, flag, aff, xs, last, block):
@@ -321,9 +342,15 @@
             pl.BlockSpec((1, tile_rows, block), lambda c, i: (c, 0, i)),
         ]
         + x_specs,
-        out_specs=pl.BlockSpec((tile_rows, width), lambda c, i: (0, 0)),
+        out_specs=pl.BlockSpec(memory_space=pl.ANY)
+        if last
+        else pl.BlockSpec((tile_rows, width), lambda c, i: (0, 0)),
         out_shape=jax.ShapeDtypeStruct((tile_rows, width), F32 if last else BF16),
-        scratch_shapes=[VMEM((tile_rows, width), F32), VMEM((tile_rows, 128), F32)],
+        scratch_shapes=[
+            VMEM((tile_rows, width), F32),
+            VMEM((tile_rows, 128), F32),
+            pltpu.SemaphoreType.DMA((4,)),
+        ],
         cost_estimate=pl.CostEstimate(
             flops=4 * slots * tile_rows * width, bytes_accessed=16 << 20, transcendentals=0
         ),
@@ -386,7 +413,7 @@
     tile_rows = centroids.shape[0]
     capacity = 2 * rows_dev // devices
     sent, late, marks, place, tiles = pack(
-        rows, block_ids, centroids, pairing, groups, members, capacity, 4
+        rows, block_ids, centroids, pairing, groups, members, capacity, 2
     )
 
     def exchanged(value, slots):

time: 195 us -> 194 us (level)
  no operation moved by 1% of the time
where the time goes in v5:
time: 194 us; the launch traced here: 192 us
  blocking collectives  86.4 us (45%)
  Pallas kernels  61.9 us (32%)
  waiting for transfers between devices  24.5 us (13%)
  starting transfers between devices  16 us (8%)
  between operations  2.03 us (1%)
    all_to_all x1, blocking collectives, exchanged(): lax.all_to_all(value.reshape(devices, -1, value.shape[-1]), ('dp', 'blk')...  86.4 us
    pallas_call x3, Pallas kernels, affinity(): pl.pallas_call(functools.partial(kernel, inner), grid=(kinds, slots // bl...  25.3 us
    pallas_call x2, Pallas kernels, sums(): pl.pallas_call(functools.partial(sums_kernel, last), grid=(2, steps), in_...  24.7 us
    all_to_all x2, waiting for transfers between devices, exchanged(): lax.all_to_all(value.reshape(devices, -1, value.shape[-1]), ('dp', 'blk')...  20 us
    all_to_all x2, starting transfers between devices, exchanged(): lax.all_to_all(value.reshape(devices, -1, value.shape[-1]), ('dp', 'blk')...  12.6 us
    pallas_call x1, Pallas kernels, pack(): pl.pallas_call(functools.partial(pack_kernel, capacity), grid=(steps,), i...  9.93 us
    ppermute x2, waiting for transfers between devices, branch(): lax.ppermute(current, 'blk', [(i, i ^ apart) for i in range(width)])  4.5 us
  transfers between devices with their start and end apart: 4, of which 3 were waited for; matrix products, arithmetic and copies ran while one was open for 0% of the time, Pallas kernels for 17%

profile of v5, /device:TPU:1, one launch (start us, length us, event | category | flops | bytes accessed | tf_op | source)
XLA Modules:
  0.0 191.6 jit_solution(13350035445172698005)
XLA Ops:
  0.6 9.9 %pack.1 = (bf16[8,16,2,16,768]{4,3,2,1,0:T(8,128)(2,1)}, bf16[8,16,16,768]{3,2,1,0:T(8,128)(2,1)}, bf16[128,1024]{1,0:T(8,128)(2,1)}, s32[1,1024]{1,0:T(1,128)}, bf16[1024,768]{1,0:T(8,128)(2,1)}) custom-call(s32[2]{0:T(128)} %pair_ref.2, s32[1,1024]{1,0:T(1,128)} %bitcast.17, bf16[1024,768]{1,0:T(8,128)(2,1)} %rows_ref.1, f32[1024,768]{1,0:T(8,128)} %tiles_ref.1), custom_call_target="tpu_custom_call" | custom-call | flops 3221225472 | bytes 20971520 | tf_op jit(solution)/shard_map/pack/pallas_call | solution.py:112
  10.6 0.0 copy-start
  10.6 86.4 %all_to_all.15 = bf16[128,32,768]{2,1,0:T(8,128)(2,1)} all-to-all(bf16[128,32,768]{2,1,0:T(8,128)(2,1)} %bitcast.14), channel_id=1, replica_groups=mesh['dp'=8,'blk'=16] {'dp','blk'}, dimensions={0} | all-to-all | bytes 12582912 | tf_op jit(solution)/shard_map/all_to_all | solution.py:420
  97.0 0.0 copy-done
  97.0 0.6 fusion
  97.6 11.3 %affinity.3 = (bf16[2,1024,2048]{2,1,0:T(8,128)(2,1)}, f32[2,1,2048]{2,1,0:T(1,128)S(1)}, f32[2,1,2048]{2,1,0:T(1,128)}) custom-call(bf16[1024,768]{1,0:T(8,128)(2,1)} %get-tuple-element.89.tiles_ref, bf16[128,2,16,768]{3,2,1,0:T(8,128)(2,1)} %bitcast.10), custom_call_target="tpu_custom_call" | custom-call | flops 6442450944 | bytes 16777216 | tf_op jit(solution)/shard_map/affinity/pallas_call | solution.py:247
  109.6 5.2 %conditional.2 = (f32[2,1,2048]{2,1,0:T(1,128)}) conditional(s32[]{:T(128)} %bitcast.3, f32[2,1,2048]{2,1,0:T(1,128)S(1)} %get-tuple-element.92.total_ref, f32[2,1,2048]{2,1,0:T(1,128)S(1)} %get-tuple-element.92.total_ref, f32[2,1,2048]{2,1,0:T(1,128)S(1)} %get-tuple-element.92.total_ref, ...), branch_computations={%region_0.0_spmd, %region_1.0_spmd, %region_2.0_spmd, %region_3.0_... | conditional | bytes 65584 | solution.py:405
  109.6 1.9 %collective-permute-start.8 = (f32[2,1,2048]{2,1,0:T(1,128)S(1)}, f32[2,1,2048]{2,1,0:T(1,128)}, u32[]{:S(2)}, u32[]{:S(2)}) collective-permute-start(f32[2,1,2048]{2,1,0:T(1,128)S(1)} %param.9), channel_id=1, source_target_pairs={{0,9},{1,8},{2,11},{3,10},{4,13},{5,12},{6,15},{7,14},{8,1},{9,0},... | collective-permute-start | bytes 49160 | tf_op jit(solution)/shard_map/cond/branch_9_fun/ppermute | solution.py:403
  111.6 3.2 %collective-permute-done.8 = f32[2,1,2048]{2,1,0:T(1,128)} collective-permute-done((f32[2,1,2048]{2,1,0:T(1,128)S(1)}, f32[2,1,2048]{2,1,0:T(1,128)}, u32[]{:S(2)}, u32[]{:S(2)}) %collective-permute-start.8) | collective-permute-done | bytes 16416 | tf_op jit(solution)/shard_map/cond/branch_9_fun/ppermute | solution.py:403
  114.8 6.1 %all-to-all-start.1 = ((bf16[128,16,768]{2,1,0:T(8,128)(2,1)}), bf16[128,16,768]{2,1,0:T(8,128)(2,1)S(1)}, u32[]{:S(2)}, u32[]{:S(2)}) async-start(bf16[128,16,768]{2,1,0:T(8,128)(2,1)} %bitcast.15), calls=%async_computation.1 | async-start | bytes 6291456 | tf_op jit(solution)/shard_map/all_to_all | solution.py:420
  121.6 12.5 %sums.2.tiles_ref = bf16[1024,768]{1,0:T(8,128)(2,1)} custom-call(bf16[1024,768]{1,0:T(8,128)(2,1)} %get-tuple-element.89.tiles_ref, f32[2,1,2048]{2,1,0:T(1,128)S(1)} %get-tuple-element.92.total_ref, f32[2,1,2048]{2,1,0:T(1,128)} %get-tuple-element.112.swapped_ref, f32[2,1,2048]{2,1,0:T(1,128)} %get-tuple-element.96.flag_ref.own_flag_ref, ...), custom_call_target="tpu_custom_call" | custom-call | flops 6442450944 | bytes 16777216 | tf_op jit(solution)/shard_map/sums/pallas_call | solution.py:334
  134.1 7.1 %affinity.4 = (bf16[2,1024,2048]{2,1,0:T(8,128)(2,1)}, f32[1,1,2048]{2,1,0:T(1,128)}, f32[128,1,128]{2,1,0:T(1,128)}) custom-call(bf16[1024,768]{1,0:T(8,128)(2,1)} %sums.2.tiles_ref, bf16[128,2,16,768]{3,2,1,0:T(8,128)(2,1)} %bitcast.12), custom_call_target="tpu_custom_call" | custom-call | flops 3221225472 | bytes 8388608 | tf_op jit(solution)/shard_map/affinity/pallas_call | solution.py:247
  141.2 20.0 %all-to-all-done.1 = bf16[128,16,768]{2,1,0:T(8,128)(2,1)S(1)} async-done(((bf16[128,16,768]{2,1,0:T(8,128)(2,1)}), bf16[128,16,768]{2,1,0:T(8,128)(2,1)S(1)}, u32[]{:S(2)}, u32[]{:S(2)}) %all-to-all-start.1) | async-done | bytes 3145760 | tf_op jit(solution)/shard_map/all_to_all | solution.py:420
  161.3 6.9 %affinity.5 = (bf16[2,1024,2048]{2,1,0:T(8,128)(2,1)}, f32[2,1,2048]{2,1,0:T(1,128)S(1)}, f32[2,1,2048]{2,1,0:T(1,128)}, f32[128,1,256]{2,1,0:T(1,128)}) custom-call(bf16[1024,768]{1,0:T(8,128)(2,1)} %sums.2.tiles_ref, bf16[128,1,16,768]{3,2,1,0:T(8,128)(2,1)S(1)} %bitcast.8, ...), custom_call_target="tpu_custom_call", output_to_operand_aliasing={{0}: (5, {})} | custom-call | flops 3221225472 | bytes 8388608 | tf_op jit(solution)/shard_map/affinity/pallas_call | solution.py:247
  168.2 2.7 %conditional.3 = (f32[2,1,2048]{2,1,0:T(1,128)}) conditional(s32[]{:T(128)} %bitcast.6, f32[2,1,2048]{2,1,0:T(1,128)S(1)} %get-tuple-element.102.total_ref, f32[2,1,2048]{2,1,0:T(1,128)S(1)} %get-tuple-element.102.total_ref, f32[2,1,2048]{2,1,0:T(1,128)S(1)} %get-tuple-element.102.total_ref, ...), branch_computations={%region_16.0_spmd, %region_17.0_spmd, %region_18.0_spmd, %region_1... | conditional | bytes 65584 | solution.py:405
  168.2 1.4 collective-permute-start.18
  169.6 1.3 collective-permute-done.18
  170.9 6.5 %all-to-all-start.2 = ((f32[128,1,256]{2,1,0:T(1,128)}), f32[128,1,256]{2,1,0:T(1,128)S(1)}, u32[]{:S(2)}, u32[]{:S(2)}) async-start(f32[128,1,256]{2,1,0:T(1,128)} %get-tuple-element.107), calls=%async_computation.2 | async-start | bytes 262144 | tf_op jit(solution)/shard_map/all_to_all | solution.py:420
  177.4 12.2 %sums.3 = f32[1024,768]{1,0:T(8,128)} custom-call(bf16[1024,768]{1,0:T(8,128)(2,1)} %sums.2.tiles_ref, f32[2,1,2048]{2,1,0:T(1,128)S(1)} %get-tuple-element.102.total_ref, f32[2,1,2048]{2,1,0:T(1,128)} %get-tuple-element.113.swapped_ref, f32[2,1,2048]{2,1,0:T(1,128)} %get-tuple-element.105.flag_ref, bf16[2,1024,2048]{2,1,0:T(8,128)(2,1)} %get-tuple-element.106.aff_ref, ...), custom_call_target="tpu_custom_call" | custom-call | flops 6442450944 | bytes 16777216 | tf_op jit(solution)/shard_map/sums/pallas_call | solution.py:334
  189.6 0.0 all-to-all-done.2.back_ref
  189.6 2.0 %energies.1 = f32[1,1024]{1,0:T(1,128)} custom-call(s32[2]{0:T(128)} %pair_ref.2, f32[128,1,256]{2,1,0:T(1,128)S(1)} %all-to-all-done.2.back_ref, bf16[128,1024]{1,0:T(8,128)(2,1)} %get-tuple-element.108.marks_ref, s32[1,1024]{1,0:T(1,128)} %get-tuple-element.109.place_ref), custom_call_target="tpu_custom_call" | custom-call | tf_op jit(solution)/shard_map/energies/pallas_call | solution.py:390
Async XLA Ops:
  10.6 86.5 %copy-start = (s32[2]{0:T(128)S(1)}, s32[2]{0:T(128)}, u32[]{:S(2)}) copy-start(s32[2]{0:T(128)} %pair_ref.2) | copy-start | bytes 28
  109.6 5.2 %collective-permute-start.8 = (f32[2,1,2048]{2,1,0:T(1,128)S(1)}, f32[2,1,2048]{2,1,0:T(1,128)}, u32[]{:S(2)}, u32[]{:S(2)}) collective-permute-start(f32[2,1,2048]{2,1,0:T(1,128)S(1)} %param.9), channel_id=1, source_target_pairs={{0,9},{1,8},{2,11},{3,10},{4,13},{5,12},{6,15},{7,14},{8,1},{9,0},... | collective-permute-start | bytes 49160 | tf_op jit(solution)/shard_map/cond/branch_9_fun/ppermute | solution.py:403
  114.8 46.5 %all-to-all-start.1 = ((bf16[128,16,768]{2,1,0:T(8,128)(2,1)}), bf16[128,16,768]{2,1,0:T(8,128)(2,1)S(1)}, u32[]{:S(2)}, u32[]{:S(2)}) async-start(bf16[128,16,768]{2,1,0:T(8,128)(2,1)} %bitcast.15), calls=%async_computation.1 | async-start | bytes 6291456 | tf_op jit(solution)/shard_map/all_to_all | solution.py:420
  168.2 2.7 %collective-permute-start.18 = (f32[2,1,2048]{2,1,0:T(1,128)S(1)}, f32[2,1,2048]{2,1,0:T(1,128)}, u32[]{:S(2)}, u32[]{:S(2)}) collective-permute-start(f32[2,1,2048]{2,1,0:T(1,128)S(1)} %param.20), channel_id=1, source_target_pairs={{0,4},{1,5},{2,6},{3,7},{4,0},{5,1},{6,2},{7,3},{8,12},{9,13},{10,... | collective-permute-start | bytes 49160 | tf_op jit(solution)/shard_map/cond/branch_4_fun/ppermute | solution.py:403
  170.9 18.7 %all-to-all-start.2 = ((f32[128,1,256]{2,1,0:T(1,128)}), f32[128,1,256]{2,1,0:T(1,128)S(1)}, u32[]{:S(2)}, u32[]{:S(2)}) async-start(f32[128,1,256]{2,1,0:T(1,128)} %get-tuple-element.107), calls=%async_computation.2 | async-start | bytes 262144 | tf_op jit(solution)/shard_map/all_to_all | solution.py:420

commit v6 on v5

--- a/solution.py
+++ b/solution.py
@@ -248,7 +248,9 @@
         functools.partial(kernel, inner),
         grid=(kinds, slots // block),
         in_specs=[
-            pl.BlockSpec((tile_rows, width), lambda c, i: (0, 0)),
+            pl.BlockSpec(memory_space=VMEM)
+            if kernel is first_kernel
+            else pl.BlockSpec((tile_rows, width), lambda c, i: (0, 0)),
             x_spec,
         ]
         + extra_specs,
@@ -428,7 +430,8 @@
 
     got = exchanged(sent, 2)
     got, pairing = lax.optimization_barrier((got, pairing))
-    aff, total, flag = affinity(first_kernel, tiles, got, 2, (), 1024, 512)
+    near = pltpu.with_memory_space_constraint(tiles, VMEM)
+    aff, total, flag = affinity(first_kernel, near, got, 2, (), 1024, 512)
     swapped = partner_swap(total, pairing[0], members)
     swapped, late = lax.optimization_barrier((swapped, late))
     got_late = pltpu.with_memory_space_constraint(exchanged(late, 1), VMEM)

time: 194 us -> 193 us (level); the launches traced: 192 us -> 193 us
  transfers between devices with their start and end apart: 4 -> 4, of which waited for: 3 -> 3; matrix products, arithmetic and copies ran while one was open for 0% -> 0% of each run, Pallas kernels for 17% -> 16%
where the time goes in v6:
time: 193 us
  blocking collectives  86.4 us (45%)
  Pallas kernels  61.4 us (32%)
  waiting for transfers between devices  26.4 us (14%)
  starting transfers between devices  16.6 us (9%)
    all_to_all x1, blocking collectives, exchanged(): lax.all_to_all(value.reshape(devices, -1, value.shape[-1]), ('dp', 'blk')...  86.4 us
    pallas_call x3, Pallas kernels, affinity(): pl.pallas_call(functools.partial(kernel, inner), grid=(kinds, slots // bl...  24.9 us
    pallas_call x2, Pallas kernels, sums(): pl.pallas_call(functools.partial(sums_kernel, last), grid=(2, steps), in_...  24.7 us
    all_to_all x2, waiting for transfers between devices, exchanged(): lax.all_to_all(value.reshape(devices, -1, value.shape[-1]), ('dp', 'blk')...  20.1 us
    all_to_all x2, starting transfers between devices, exchanged(): lax.all_to_all(value.reshape(devices, -1, value.shape[-1]), ('dp', 'blk')...  12.6 us
    pallas_call x1, Pallas kernels, pack(): pl.pallas_call(functools.partial(pack_kernel, capacity), grid=(steps,), i...  9.85 us
    ppermute x2, waiting for transfers between devices, branch(): lax.ppermute(current, 'blk', [(i, i ^ apart) for i in range(width)])  6.36 us
    ppermute x2, starting transfers between devices, branch(): lax.ppermute(current, 'blk', [(i, i ^ apart) for i in range(width)])  3.91 us
  transfers between devices with their start and end apart: 4, of which 3 were waited for; matrix products, arithmetic and copies ran while one was open for 0% of the time, Pallas kernels for 16%

profile of v6, /device:TPU:1, one launch (start us, length us, event | category | flops | bytes accessed | tf_op | source)
XLA Modules:
  0.0 193.3 jit_solution(13227939110202635775)
XLA Ops:
  0.6 9.8 %pack.1 = (bf16[8,16,2,16,768]{4,3,2,1,0:T(8,128)(2,1)}, bf16[8,16,16,768]{3,2,1,0:T(8,128)(2,1)}, bf16[128,1024]{1,0:T(8,128)(2,1)}, s32[1,1024]{1,0:T(1,128)}, bf16[1024,768]{1,0:T(8,128)(2,1)}) custom-call(s32[2]{0:T(128)} %pair_ref.2, s32[1,1024]{1,0:T(1,128)} %bitcast.17, bf16[1024,768]{1,0:T(8,128)(2,1)} %rows_ref.1, f32[1024,768]{1,0:T(8,128)} %tiles_ref.1), custom_call_target="tpu_custom_call" | custom-call | flops 3221225472 | bytes 20971520 | tf_op jit(solution)/shard_map/pack/pallas_call | solution.py:112
  10.5 0.0 copy-start.1
  10.5 0.0 copy-start
  10.5 86.4 %all_to_all.15 = bf16[128,32,768]{2,1,0:T(8,128)(2,1)} all-to-all(bf16[128,32,768]{2,1,0:T(8,128)(2,1)} %bitcast.14), channel_id=1, replica_groups=mesh['dp'=8,'blk'=16] {'dp','blk'}, dimensions={0} | all-to-all | bytes 12582912 | tf_op jit(solution)/shard_map/all_to_all | solution.py:422
  96.9 0.0 copy-done.1
  96.9 0.6 fusion
  97.5 0.0 copy-done
  97.5 10.8 %affinity.3 = (bf16[2,1024,2048]{2,1,0:T(8,128)(2,1)}, f32[2,1,2048]{2,1,0:T(1,128)S(1)}, f32[2,1,2048]{2,1,0:T(1,128)}) custom-call(bf16[1024,768]{1,0:T(8,128)(2,1)S(1)} %copy-done, bf16[128,2,16,768]{3,2,1,0:T(8,128)(2,1)} %bitcast.10), custom_call_target="tpu_custom_call" | custom-call | flops 6442450944 | bytes 16777216 | tf_op jit(solution)/shard_map/affinity/pallas_call | solution.py:247
  108.9 5.2 %conditional.2 = (f32[2,1,2048]{2,1,0:T(1,128)}) conditional(s32[]{:T(128)} %bitcast.3, f32[2,1,2048]{2,1,0:T(1,128)S(1)} %get-tuple-element.92.total_ref, f32[2,1,2048]{2,1,0:T(1,128)S(1)} %get-tuple-element.92.total_ref, f32[2,1,2048]{2,1,0:T(1,128)S(1)} %get-tuple-element.92.total_ref, ...), branch_computations={%region_0.0_spmd, %region_1.0_spmd, %region_2.0_spmd, %region_3.0_... | conditional | bytes 65584 | solution.py:407
  109.0 1.9 %collective-permute-start.8 = (f32[2,1,2048]{2,1,0:T(1,128)S(1)}, f32[2,1,2048]{2,1,0:T(1,128)}, u32[]{:S(2)}, u32[]{:S(2)}) collective-permute-start(f32[2,1,2048]{2,1,0:T(1,128)S(1)} %param.9), channel_id=1, source_target_pairs={{0,9},{1,8},{2,11},{3,10},{4,13},{5,12},{6,15},{7,14},{8,1},{9,0},... | collective-permute-start | bytes 49160 | tf_op jit(solution)/shard_map/cond/branch_9_fun/ppermute | solution.py:405
  110.9 3.2 %collective-permute-done.8 = f32[2,1,2048]{2,1,0:T(1,128)} collective-permute-done((f32[2,1,2048]{2,1,0:T(1,128)S(1)}, f32[2,1,2048]{2,1,0:T(1,128)}, u32[]{:S(2)}, u32[]{:S(2)}) %collective-permute-start.8) | collective-permute-done | bytes 16416 | tf_op jit(solution)/shard_map/cond/branch_9_fun/ppermute | solution.py:405
  114.1 6.1 %all-to-all-start.1 = ((bf16[128,16,768]{2,1,0:T(8,128)(2,1)}), bf16[128,16,768]{2,1,0:T(8,128)(2,1)S(1)}, u32[]{:S(2)}, u32[]{:S(2)}) async-start(bf16[128,16,768]{2,1,0:T(8,128)(2,1)} %bitcast.15), calls=%async_computation.1 | async-start | bytes 6291456 | tf_op jit(solution)/shard_map/all_to_all | solution.py:422
  120.9 12.5 %sums.2.tiles_ref = bf16[1024,768]{1,0:T(8,128)(2,1)} custom-call(bf16[1024,768]{1,0:T(8,128)(2,1)} %get-tuple-element.89.tiles_ref, f32[2,1,2048]{2,1,0:T(1,128)S(1)} %get-tuple-element.92.total_ref, f32[2,1,2048]{2,1,0:T(1,128)} %get-tuple-element.112.swapped_ref, f32[2,1,2048]{2,1,0:T(1,128)} %get-tuple-element.96.flag_ref.own_flag_ref, ...), custom_call_target="tpu_custom_call" | custom-call | flops 6442450944 | bytes 16777216 | tf_op jit(solution)/shard_map/sums/pallas_call | solution.py:336
  133.4 7.1 %affinity.4 = (bf16[2,1024,2048]{2,1,0:T(8,128)(2,1)}, f32[1,1,2048]{2,1,0:T(1,128)}, f32[128,1,128]{2,1,0:T(1,128)}) custom-call(bf16[1024,768]{1,0:T(8,128)(2,1)} %sums.2.tiles_ref, bf16[128,2,16,768]{3,2,1,0:T(8,128)(2,1)} %bitcast.12), custom_call_target="tpu_custom_call" | custom-call | flops 3221225472 | bytes 8388608 | tf_op jit(solution)/shard_map/affinity/pallas_call | solution.py:247
  140.6 20.0 %all-to-all-done.1 = bf16[128,16,768]{2,1,0:T(8,128)(2,1)S(1)} async-done(((bf16[128,16,768]{2,1,0:T(8,128)(2,1)}), bf16[128,16,768]{2,1,0:T(8,128)(2,1)S(1)}, u32[]{:S(2)}, u32[]{:S(2)}) %all-to-all-start.1) | async-done | bytes 3145760 | tf_op jit(solution)/shard_map/all_to_all | solution.py:422
  160.6 6.9 %affinity.5 = (bf16[2,1024,2048]{2,1,0:T(8,128)(2,1)}, f32[2,1,2048]{2,1,0:T(1,128)S(1)}, f32[2,1,2048]{2,1,0:T(1,128)}, f32[128,1,256]{2,1,0:T(1,128)}) custom-call(bf16[1024,768]{1,0:T(8,128)(2,1)} %sums.2.tiles_ref, bf16[128,1,16,768]{3,2,1,0:T(8,128)(2,1)S(1)} %bitcast.8, ...), custom_call_target="tpu_custom_call", output_to_operand_aliasing={{0}: (5, {})} | custom-call | flops 3221225472 | bytes 8388608 | tf_op jit(solution)/shard_map/affinity/pallas_call | solution.py:247
  167.5 5.1 %conditional.3 = (f32[2,1,2048]{2,1,0:T(1,128)}) conditional(s32[]{:T(128)} %bitcast.6, f32[2,1,2048]{2,1,0:T(1,128)S(1)} %get-tuple-element.102.total_ref, f32[2,1,2048]{2,1,0:T(1,128)S(1)} %get-tuple-element.102.total_ref, f32[2,1,2048]{2,1,0:T(1,128)S(1)} %get-tuple-element.102.total_ref, ...), branch_computations={%region_16.0_spmd, %region_17.0_spmd, %region_18.0_spmd, %region_1... | conditional | bytes 65584 | solution.py:407
  167.5 2.0 %collective-permute-start.20 = (f32[2,1,2048]{2,1,0:T(1,128)S(1)}, f32[2,1,2048]{2,1,0:T(1,128)}, u32[]{:S(2)}, u32[]{:S(2)}) collective-permute-start(f32[2,1,2048]{2,1,0:T(1,128)S(1)} %param.22), channel_id=1, source_target_pairs={{0,6},{1,7},{2,4},{3,5},{4,2},{5,3},{6,0},{7,1},{8,14},{9,15},{10,... | collective-permute-start | bytes 49160 | tf_op jit(solution)/shard_map/cond/branch_6_fun/ppermute | solution.py:405
  169.5 3.1 %collective-permute-done.20 = f32[2,1,2048]{2,1,0:T(1,128)} collective-permute-done((f32[2,1,2048]{2,1,0:T(1,128)S(1)}, f32[2,1,2048]{2,1,0:T(1,128)}, u32[]{:S(2)}, u32[]{:S(2)}) %collective-permute-start.20) | collective-permute-done | bytes 16416 | tf_op jit(solution)/shard_map/cond/branch_6_fun/ppermute | solution.py:405
  172.6 6.5 %all-to-all-start.2 = ((f32[128,1,256]{2,1,0:T(1,128)}), f32[128,1,256]{2,1,0:T(1,128)S(1)}, u32[]{:S(2)}, u32[]{:S(2)}) async-start(f32[128,1,256]{2,1,0:T(1,128)} %get-tuple-element.107), calls=%async_computation.2 | async-start | bytes 262144 | tf_op jit(solution)/shard_map/all_to_all | solution.py:422
  179.2 12.2 %sums.3 = f32[1024,768]{1,0:T(8,128)} custom-call(bf16[1024,768]{1,0:T(8,128)(2,1)} %sums.2.tiles_ref, f32[2,1,2048]{2,1,0:T(1,128)S(1)} %get-tuple-element.102.total_ref, f32[2,1,2048]{2,1,0:T(1,128)} %get-tuple-element.113.swapped_ref, f32[2,1,2048]{2,1,0:T(1,128)} %get-tuple-element.105.flag_ref, bf16[2,1024,2048]{2,1,0:T(8,128)(2,1)} %get-tuple-element.106.aff_ref, ...), custom_call_target="tpu_custom_call" | custom-call | flops 6442450944 | bytes 16777216 | tf_op jit(solution)/shard_map/sums/pallas_call | solution.py:336
  191.3 0.0 all-to-all-done.2.back_ref
  191.4 2.0 %energies.1 = f32[1,1024]{1,0:T(1,128)} custom-call(s32[2]{0:T(128)} %pair_ref.2, f32[128,1,256]{2,1,0:T(1,128)S(1)} %all-to-all-done.2.back_ref, bf16[128,1024]{1,0:T(8,128)(2,1)} %get-tuple-element.108.marks_ref, s32[1,1024]{1,0:T(1,128)} %get-tuple-element.109.place_ref), custom_call_target="tpu_custom_call" | custom-call | tf_op jit(solution)/shard_map/energies/pallas_call | solution.py:392
Async XLA Ops:
  10.5 86.5 %copy-start.1 = (s32[2]{0:T(128)S(1)}, s32[2]{0:T(128)}, u32[]{:S(2)}) copy-start(s32[2]{0:T(128)} %pair_ref.2) | copy-start | bytes 28
  10.5 87.0 %copy-start = (bf16[1024,768]{1,0:T(8,128)(2,1)S(1)}, bf16[1024,768]{1,0:T(8,128)(2,1)}, u32[]{:S(2)}) copy-start(bf16[1024,768]{1,0:T(8,128)(2,1)} %get-tuple-element.89.tiles_ref) | copy-start | bytes 4718596
  109.0 5.2 %collective-permute-start.8 = (f32[2,1,2048]{2,1,0:T(1,128)S(1)}, f32[2,1,2048]{2,1,0:T(1,128)}, u32[]{:S(2)}, u32[]{:S(2)}) collective-permute-start(f32[2,1,2048]{2,1,0:T(1,128)S(1)} %param.9), channel_id=1, source_target_pairs={{0,9},{1,8},{2,11},{3,10},{4,13},{5,12},{6,15},{7,14},{8,1},{9,0},... | collective-permute-start | bytes 49160 | tf_op jit(solution)/shard_map/cond/branch_9_fun/ppermute | solution.py:405
  114.1 46.5 %all-to-all-start.1 = ((bf16[128,16,768]{2,1,0:T(8,128)(2,1)}), bf16[128,16,768]{2,1,0:T(8,128)(2,1)S(1)}, u32[]{:S(2)}, u32[]{:S(2)}) async-start(bf16[128,16,768]{2,1,0:T(8,128)(2,1)} %bitcast.15), calls=%async_computation.1 | async-start | bytes 6291456 | tf_op jit(solution)/shard_map/all_to_all | solution.py:422
  167.5 5.1 %collective-permute-start.20 = (f32[2,1,2048]{2,1,0:T(1,128)S(1)}, f32[2,1,2048]{2,1,0:T(1,128)}, u32[]{:S(2)}, u32[]{:S(2)}) collective-permute-start(f32[2,1,2048]{2,1,0:T(1,128)S(1)} %param.22), channel_id=1, source_target_pairs={{0,6},{1,7},{2,4},{3,5},{4,2},{5,3},{6,0},{7,1},{8,14},{9,15},{10,... | collective-permute-start | bytes 49160 | tf_op jit(solution)/shard_map/cond/branch_6_fun/ppermute | solution.py:405
  172.6 18.7 %all-to-all-start.2 = ((f32[128,1,256]{2,1,0:T(1,128)}), f32[128,1,256]{2,1,0:T(1,128)S(1)}, u32[]{:S(2)}, u32[]{:S(2)}) async-start(f32[128,1,256]{2,1,0:T(1,128)} %get-tuple-element.107), calls=%async_computation.2 | async-start | bytes 262144 | tf_op jit(solution)/shard_map/all_to_all | solution.py:422
